TPU v7x, 256 devices: a whole 4x4x8 slice. The times are simulated.
256 devices in a mesh: state: 16 (over x, y), sample: 16 (over z, core).
Axes of the slice: x: 4, y: 4, z: 8, core: 2. Of those that a mesh axis runs over, the one named last changes fastest.
Arguments:
- energy: bfloat16 [32, 524288], P(None, 'sample'), may hold values from -28 to 28
- coef: bfloat16 [32, 4096], P(None, 'state'), may hold values from -6 to 6
- anchor: int32 [524288], P('sample'), may hold values from 0 to 4096, as said below
- f_start: float32 [4096], P('state'), may hold values from -8 to 8
Outputs:
- free_energy: float32 [4096], P('state')
Inputs may be any that keep to these rules, and one draw needn't show every extreme that they name: anchor_n is the state whose evolution drew slot n; the value 4096 marks an empty slot. On each index of the sample axis the live slots come first among its 32768 slots; all indices together hold exactly 196608 live slots, and on some index all 32768 slots are live. Every state is the anchor of at least one live slot.
All inputs are finite; a program needn't handle non-finite values.
Results may differ from a plain program's by a relative error of at most 0.0003.
Values may be sent and summed in bfloat16 or wider, within the bound.
No kernel may reach another device: no remote copies, remote signals or barrier semaphores. Data moves between devices by JAX's collectives and lax.ppermute only.
A program may use at most 64 MiB of HBM per device.

v0:
```python
import jax
import jax.numpy as jnp
from jax import lax
from jax.sharding import PartitionSpec as P

ITERS = 2


low_value = -1e30


def merged(value, axis, combine):
    everything = jax.tree.map(lambda part: lax.all_gather(part, axis), value)
    leading = jax.tree.map(lambda part: part[0], everything)

    def turn(k, so_far):
        return combine(so_far, jax.tree.map(lambda part: part[k], everything))

    return lax.fori_loop(1, lax.axis_size(axis), turn, leading)


def block_size(columns):
    for length in (4096, 2048, 1024, 512, 256, 128):
        return length
    return columns


def pair_merge(former, latter):
    highest = jnp.maximum(former[0], latter[0])
    return (
        highest,
        former[1] * jnp.exp(former[0] - highest) + latter[1] * jnp.exp(latter[0] - highest),
    )


def potentials(coef_part, tile_data):
    return lax.dot_general(
        coef_part, tile_data, (((0,), (0,)), ((), ())), preferred_element_type=jnp.float32
    )


def column_terms(log_weight, potential):
    scores = log_weight[:, None] - potential
    highest = jnp.max(scores, axis=0)
    return (highest, jnp.sum(jnp.exp(scores - highest[None, :]), axis=0))


def row_terms(running, potential, log_denom, live_part):
    weighted = jnp.where(live_part[None, :], -potential - log_denom[None, :], low_value)
    highest = jnp.max(weighted, axis=1)
    summed = jnp.sum(
        jnp.where(live_part[None, :], jnp.exp(weighted - highest[:, None]), 0.0), axis=1
    )
    return pair_merge(running, (highest, summed))


def working_set(energy, anchor, states):
    live_mask = anchor < states
    return (energy, live_mask)


def center(unshifted, states):
    summed = lax.psum(jnp.sum(unshifted), "state")
    return unshifted - summed / states


def per_device(energy, coef, anchor, f_start):
    state_rows = coef.shape[1]
    groups = lax.axis_size("state")
    states = state_rows * groups
    row_start = lax.axis_index("state") * state_rows
    work_data, work_mask = working_set(energy, anchor, states)
    histogram = jax.ops.segment_sum(
        jnp.ones(anchor.shape, jnp.float32), anchor, num_segments=states + 1
    )[:states]
    histogram = lax.dynamic_slice_in_dim(histogram, row_start, state_rows)
    counts = lax.psum(histogram, "sample")
    log_counts = jnp.log(counts)
    estimate = f_start
    column_total = work_data.shape[1]
    block_len = block_size(column_total)
    block_total = column_total // block_len
    for iteration in range(ITERS):
        log_weight = log_counts + estimate

        def column_pass(block_index, running):
            tile_data = lax.dynamic_slice_in_dim(work_data, block_index * block_len, block_len, 1)
            highest, summed = column_terms(log_weight, potentials(coef, tile_data))
            return (
                lax.dynamic_update_slice_in_dim(running[0], highest, block_index * block_len, 0),
                lax.dynamic_update_slice_in_dim(running[1], summed, block_index * block_len, 0),
            )

        empty_cols = (
            jnp.zeros((column_total,), jnp.float32),
            jnp.zeros((column_total,), jnp.float32),
        )
        col_high, col_sum = lax.fori_loop(0, block_total, column_pass, empty_cols)
        col_high, col_sum = merged((col_high, col_sum), "state", pair_merge)
        log_denom = col_high + jnp.log(col_sum)

        def row_pass(block_index, running):
            tile_data = lax.dynamic_slice_in_dim(work_data, block_index * block_len, block_len, 1)
            live_part = lax.dynamic_slice_in_dim(work_mask, block_index * block_len, block_len)
            denom_part = lax.dynamic_slice_in_dim(log_denom, block_index * block_len, block_len)
            return row_terms(running, potentials(coef, tile_data), denom_part, live_part)

        initial = (
            jnp.full((state_rows,), low_value, jnp.float32),
            jnp.zeros((state_rows,), jnp.float32),
        )
        row_high, row_sum = lax.fori_loop(0, block_total, row_pass, initial)
        row_high, row_sum = merged((row_high, row_sum), "sample", pair_merge)
        unshifted = -(row_high + jnp.log(row_sum))
        estimate = center(unshifted, states)
    return estimate


def solution(mesh):
    in_specs = (P(None, "sample"), P(None, "state"), P("sample"), P("state"))
    out_specs = P("state")
    return jax.shard_map(
        per_device, mesh=mesh, in_specs=in_specs, out_specs=out_specs, check_vma=False
    )
```

profile of v0, /device:TPU:1, one launch (start us, length us, event | category | flops | bytes accessed | tf_op | source)
XLA Modules:
  0.0 788.8 jit_solution(18265833568782395056)
XLA Ops:
  6.5 203.8 %scatter_custom_fusion = f32[4097]{0:T(1024)S(1)} fusion(s32[32768]{0:T(1024)} %param.22, f32[32768]{0:T(1024)S(1)} %broadcast.42, f32[]{:T(128)} %constant.331.clone.1), kind=kCustom, calls=%fused_computation.48 | custom fusion | flops 32768 | bytes 16900 | tf_op jit(solution)/shard_map/scatter-add | solution.py:73
  210.4 39.4 %psum.21 = f32[256]{0:T(256)S(1)} all-reduce(f32[256]{0:T(256)S(1)} %dynamic_slice.139), channel_id=1, replica_groups=mesh['state'=16,'sample'=16] {'sample'}, use_global_device_ids=true, to_apply=%region_1.0 | all-reduce | flops 256 | bytes 2048 | tf_op jit(solution)/shard_map/psum | solution.py:77
  250.6 25.1 %while.130 = (s32[]{:T(128)}, f32[32768]{0:T(1024)S(1)}, f32[32768]{0:T(1024)S(1)}, f32[256]{0:T(256)S(1)}, bf16[32,32768]{1,0:T(8,128)(2,1)}, /*index=5*/bf16[3...) while((s32[]{:T(128)}, f32[32768]{0:T(1024)S(1)}, f32[32768]{0:T(1024)S(1)}, ...), condition=%wide.region_5.0_spmd, body=%wide.region_2.0_spmd.sunk | while | flops 71294984 | bytes 8783007 | solution.py:98
  277.3 52.6 %all-gather.17.cloned.1.call-done = f32[524288]{0:T(1024)} async-done(((f32[32768]{0:T(1024)}), f32[524288]{0:T(1024)}) %all-gather.17.cloned.1.call-update) | async-done | bytes 2097168 | tf_op jit(solution)/shard_map/all_gather | solution.py:13
  331.7 50.0 %all-gather.19.cloned.1.call-done = f32[524288]{0:T(1024)} async-done(((f32[32768]{0:T(1024)}), f32[524288]{0:T(1024)}) %all-gather.19.cloned.1.call-update) | async-done | bytes 2097168 | tf_op jit(solution)/shard_map/all_gather | solution.py:13
  384.6 23.3 %while.131 = (s32[]{:T(128)}, f32[32768]{0:T(1024)S(1)}, f32[32768]{0:T(1024)S(1)}, f32[16,32768]{1,0:T(8,128)S(1)}, f32[16,32768]{1,0:T(8,128)}, /*index=5*/s32[]{:T(128)}, s32[]{:T(128)}, s32[]{:T(128)}) while((s32[]{:T(128)}, f32[32768]{0:T(1024)S(1)}, f32[32768]{0:T(1024)S(1)}, f32[16,32768]{1,0:T(8,128)S(1)}, f32[16,32768]{1,0:T(8,128)}, ...), condition=%wide.region_7.0_spmd, body=%wide.region_6.0_spmd.sunk | while | flops 196613 | bytes 1310843 | solution.py:19
  407.9 41.9 %while.136 = (s32[]{:T(128)}, f32[256]{0:T(256)S(1)}, f32[256]{0:T(256)S(1)}, pred[32768]{0:T(1024)(128)(4,1)S(1)}, bf16[32,32768]{1,0:T(8,128)(2,1)}, /*index=5...) while((s32[]{:T(128)}, f32[256]{0:T(256)S(1)}, ...), condition=%wide.region_11.12_spmd.clone, body=%wide.region_8.11_spmd.clone.sunk | while | flops 74450440 | bytes 8742073 | solution.py:112
  408.0 3.0 fusion.45
  413.2 3.0 fusion.45
  434.1 3.0 fusion.45
  439.4 3.0 fusion.45
  449.8 18.8 %all-gather.8 = f32[16,1,256]{2,1,0:T(1,128)S(1)} all-gather(f32[1,1,256]{2,1,0:T(1,128)S(1)} %bitcast.69), channel_id=4, replica_groups=mesh['state'=16,'sample'=16] {'sample'}, dimensions={0}, use_global_device_ids=true | all-gather | bytes 17408 | tf_op jit(solution)/shard_map/all_gather | solution.py:13
  468.6 15.0 %all-gather.9 = f32[16,1,256]{2,1,0:T(1,128)S(1)} all-gather(f32[1,1,256]{2,1,0:T(1,128)S(1)} %bitcast.68), channel_id=5, replica_groups=mesh['state'=16,'sample'=16] {'sample'}, dimensions={0}, use_global_device_ids=true | all-gather | bytes 17408 | tf_op jit(solution)/shard_map/all_gather | solution.py:13
  485.7 31.6 %psum.22 = f32[]{:T(128)} all-reduce(f32[]{:T(128)S(6)} %neg.27), channel_id=1, replica_groups=mesh['state'=16,'sample'=16] {'state'}, use_global_device_ids=true, to_apply=%region_15.16 | all-reduce | flops 1 | bytes 8 | tf_op jit(solution)/shard_map/psum | solution.py:63
  518.0 25.1 %while.133 = (s32[]{:T(128)}, f32[32768]{0:T(1024)S(1)}, f32[32768]{0:T(1024)S(1)}, f32[256]{0:T(256)S(1)}, bf16[32,32768]{1,0:T(8,128)(2,1)}, /*index=5*/bf16[3...) while((s32[]{:T(128)}, f32[32768]{0:T(1024)S(1)}, f32[32768]{0:T(1024)S(1)}, ...), condition=%wide.region_19.20_spmd, body=%wide.region_16.19_spmd.sunk | while | flops 71294984 | bytes 8783007 | solution.py:98
  544.4 49.5 %all-gather.21.cloned.1.call-done = f32[524288]{0:T(1024)} async-done(((f32[32768]{0:T(1024)}), f32[524288]{0:T(1024)}) %all-gather.21.cloned.1.call-update) | async-done | bytes 2097168 | tf_op jit(solution)/shard_map/all_gather | solution.py:13
  595.7 49.9 %all-gather.23.cloned.1.call-done = f32[524288]{0:T(1024)} async-done(((f32[32768]{0:T(1024)}), f32[524288]{0:T(1024)}) %all-gather.23.cloned.1.call-update) | async-done | bytes 2097168 | tf_op jit(solution)/shard_map/all_gather | solution.py:13
  648.4 23.3 %while.134 = (s32[]{:T(128)}, f32[32768]{0:T(1024)S(1)}, f32[32768]{0:T(1024)S(1)}, f32[16,32768]{1,0:T(8,128)S(1)}, f32[16,32768]{1,0:T(8,128)}, /*index=5*/s32[]{:T(128)}, s32[]{:T(128)}, s32[]{:T(128)}) while((s32[]{:T(128)}, f32[32768]{0:T(1024)S(1)}, f32[32768]{0:T(1024)S(1)}, f32[16,32768]{1,0:T(8,128)S(1)}, f32[16,32768]{1,0:T(8,128)}, ...), condition=%wide.region_21.22_spmd, body=%wide.region_20.21_spmd.sunk | while | flops 196613 | bytes 1310843 | solution.py:19
  671.7 41.9 %while.137 = (s32[]{:T(128)}, f32[256]{0:T(256)S(1)}, f32[256]{0:T(256)S(1)}, pred[32768]{0:T(1024)(128)(4,1)S(1)}, bf16[32,32768]{1,0:T(8,128)(2,1)}, /*index=5...) while((s32[]{:T(128)}, f32[256]{0:T(256)S(1)}, ...), condition=%wide.region_25.26_spmd.clone, body=%wide.region_22.25_spmd.clone.sunk | while | flops 74450440 | bytes 8742073 | solution.py:112
  671.8 3.0 fusion.48
  677.0 3.0 fusion.48
  713.7 18.7 %all-gather.10 = f32[16,1,256]{2,1,0:T(1,128)S(1)} all-gather(f32[1,1,256]{2,1,0:T(1,128)S(1)} %bitcast.71), channel_id=8, replica_groups=mesh['state'=16,'sample'=16] {'sample'}, dimensions={0}, use_global_device_ids=true | all-gather | bytes 17408 | tf_op jit(solution)/shard_map/all_gather | solution.py:13
  732.4 15.0 %all-gather.11 = f32[16,1,256]{2,1,0:T(1,128)S(1)} all-gather(f32[1,1,256]{2,1,0:T(1,128)S(1)} %bitcast.70), channel_id=9, replica_groups=mesh['state'=16,'sample'=16] {'sample'}, dimensions={0}, use_global_device_ids=true | all-gather | bytes 17408 | tf_op jit(solution)/shard_map/all_gather | solution.py:13
  749.5 31.6 %psum.23 = f32[]{:T(128)} all-reduce(f32[]{:T(128)S(6)} %neg.29), channel_id=1, replica_groups=mesh['state'=16,'sample'=16] {'state'}, use_global_device_ids=true, to_apply=%region_29.30 | all-reduce | flops 1 | bytes 8 | tf_op jit(solution)/shard_map/psum | solution.py:63
  (319 shorter events, 177.7 us)
Async XLA Ops:
  6.5 323.4 %all-gather.17.cloned.1.call-start = ((), (), s32[]{:S(2)}) async-start(), calls=%async_computation | async-start | bytes 2228224 | tf_op jit(solution)/shard_map/all_gather | solution.py:13
  250.6 26.6 %copy-start.5 = (s32[32768]{0:T(1024)S(1)}, s32[32768]{0:T(1024)}, u32[]{:S(2)}) copy-start(s32[32768]{0:T(1024)} %param.22) | copy-start | bytes 393220
  275.7 0.6 copy-start.4
  275.7 0.7 copy-start.3
  276.4 105.3 %all-gather.19.cloned.1.call-start = ((), (), s32[]{:S(2)}) async-start(), calls=%async_computation.1 | async-start | bytes 2228224 | tf_op jit(solution)/shard_map/all_gather | solution.py:13
  277.1 316.8 %all-gather.21.cloned.1.call-start = ((), (), s32[]{:S(2)}) async-start(), calls=%async_computation.2 | async-start | bytes 2228224 | tf_op jit(solution)/shard_map/all_gather | solution.py:13
  329.9 54.7 %slice-start = ((f32[524288]{0:T(1024)}), f32[32768]{0:T(1024)S(1)}, s32[]{:S(2)}) async-start(f32[524288]{0:T(1024)} %all-gather.17.cloned.1.call-done), calls=%async_computation.4 | async-start | bytes 262144 | tf_op jit(solution)/shard_map/slice | solution.py:14
  381.7 2.8 slice-start.2
  384.6 23.3 %copy-start = (bf16[32,256]{1,0:T(8,128)(2,1)S(1)}, bf16[32,256]{1,0:T(8,128)(2,1)}, u32[]{:S(2)}) copy-start(bf16[32,256]{1,0:T(8,128)(2,1)} %get-tuple-element.1764) | copy-start | bytes 49156
  543.1 0.6 copy-start.2
  543.1 0.7 copy-start.1
  543.8 101.8 %all-gather.23.cloned.1.call-start = ((), (), s32[]{:S(2)}) async-start(), calls=%async_computation.3 | async-start | bytes 2228224 | tf_op jit(solution)/shard_map/all_gather | solution.py:13
  593.9 54.5 %slice-start.1 = ((f32[524288]{0:T(1024)}), f32[32768]{0:T(1024)S(1)}, s32[]{:S(2)}) async-start(f32[524288]{0:T(1024)} %all-gather.21.cloned.1.call-done), calls=%async_computation.5 | async-start | bytes 262144 | tf_op jit(solution)/shard_map/slice | solution.py:14
  645.6 2.8 slice-start.3
Sparse Core Ops, SparseCore 0:
  276.5 53.3 all-gather.16
  332.3 49.3 all-gather.18
  543.9 49.9 all-gather.20
  596.2 49.3 all-gather.22
where the time goes:
time: 798 us; the launch traced here: 789 us
  other arithmetic  255 us (32%)
  waiting for transfers between devices  203 us (25%)
  blocking collectives  170 us (21%)
  matrix products  75.3 us (9%)
  local copies, waits for them, and re-layouts  66.3 us (8%)
  between operations  16 us (2%)
    scatter-add x1, other arithmetic, per_device(): jax.ops.segment_sum(jnp.ones(anchor.shape, jnp.float32), anchor, num_segm...  204 us
    all_gather x4, waiting for transfers between devices, merged(): everything = jax.tree.map(lambda part: lax.all_gather(part, axis), value)  202 us
    dot_general x32, matrix products, potentials(): lax.dot_general(coef_part, tile_data, (((0,), (0,)), ((), ())), preferred...  75.3 us
    all_gather x4, blocking collectives, merged(): everything = jax.tree.map(lambda part: lax.all_gather(part, axis), value)  67.5 us
    psum x2, blocking collectives, center(): summed = lax.psum(jnp.sum(unshifted), 'state')  63.2 us
    dynamic_slice x60, local copies, waits for them, and re-layouts, turn(): return combine(so_far, jax.tree.map(lambda part: part[k], everything))  42.7 us
    psum x1, blocking collectives, per_device(): counts = lax.psum(histogram, 'sample')  39.4 us
    reduce_sum x16, other arithmetic, row_terms(): jnp.sum(jnp.where(live_part[None, :], jnp.exp(weighted - highest[:, None]...  34.5 us
  transfers between devices with their start and end apart: 4, of which 4 were waited for; matrix products, arithmetic and copies ran while one was open for 0% of the time, Pallas kernels for 0%

commit v1 on v0

v1 whole, which is shorter than its diff:
```python
import functools

import jax
import jax.numpy as jnp
from jax import lax
from jax.experimental import pallas as pl
from jax.experimental.pallas import tpu as pltpu
from jax.sharding import PartitionSpec as P

ITERS = 2

LOG2E = 1.4426950408889634
LN2 = 0.6931471805599453
LOW = -1.0e30
SAFE_SUM = 1.0e-25

LANES = 128
STATE_TILE = 256
SAMPLE_TILE = 512
DEPTH = 128


def split3(value):
    high = value.astype(jnp.bfloat16).astype(jnp.float32)
    rest = value - high
    middle = rest.astype(jnp.bfloat16).astype(jnp.float32)
    low = (rest - middle).astype(jnp.bfloat16).astype(jnp.float32)
    return high, middle, low


def histogram_kernel(group_ref, anchor_ref, out_ref):
    base = group_ref[0] * 16
    total = anchor_ref.shape[1]
    step = 4096
    row = lax.broadcasted_iota(jnp.int32, (16, step), 0)
    counts = jnp.zeros((16, 16), jnp.float32)
    for start in range(0, total, step):
        anchor = anchor_ref[:, start : start + step]
        high = lax.shift_right_logical(anchor, 4) - base
        low = lax.bitwise_and(anchor, 15)
        high_hot = jnp.where(row == high, 1.0, 0.0).astype(jnp.bfloat16)
        low_hot = jnp.where(row == low, 1.0, 0.0).astype(jnp.bfloat16)
        counts += lax.dot_general(
            high_hot, low_hot, (((1,), (1,)), ((), ())), preferred_element_type=jnp.float32
        )
    lane = lax.broadcasted_iota(jnp.int32, (16, 256), 1)
    row16 = lax.broadcasted_iota(jnp.int32, (16, 256), 0)
    spread = jnp.where(lax.bitwise_and(lane, 15) == row16, 1.0, 0.0)
    placed = lax.dot_general(
        counts,
        spread,
        (((1,), (0,)), ((), ())),
        preferred_element_type=jnp.float32,
        precision=lax.Precision.HIGHEST,
    )
    flat = jnp.sum(jnp.where(lax.shift_right_logical(lane, 4) == row16, placed, 0.0), axis=0, keepdims=True)
    out_ref[...] = jnp.broadcast_to(flat[None], out_ref.shape)


def histogram(group, anchor, copies):
    total = anchor.shape[0]
    return pl.pallas_call(
        histogram_kernel,
        out_shape=jax.ShapeDtypeStruct((copies, 1, 256), jnp.float32),
        grid_spec=pltpu.PrefetchScalarGridSpec(
            num_scalar_prefetch=1,
            grid=(1,),
            in_specs=[pl.BlockSpec((1, total), lambda i, g: (0, 0))],
            out_specs=pl.BlockSpec((copies, 1, 256), lambda i, g: (0, 0, 0)),
        ),
        name="histogram",
    )(group, anchor.reshape(1, total))


def pack_kernel(counts_ref, start_ref, coef_ref, out_ref):
    counts = jnp.sum(counts_ref[...], axis=0)
    log_counts = jnp.log(counts)
    rows = list(split3(log_counts)) + list(split3(start_ref[...]))
    rows.append(jnp.zeros((2,) + counts.shape[1:], jnp.float32))
    packed = jnp.concatenate([coef_ref[...].astype(jnp.float32)] + rows, axis=0).astype(jnp.bfloat16)
    out_ref[...] = jnp.broadcast_to(packed[None], out_ref.shape)


def pack(counts, f_start, coef, copies):
    components, states = coef.shape
    return pl.pallas_call(
        pack_kernel,
        out_shape=jax.ShapeDtypeStruct((copies, components + 8, states), jnp.bfloat16),
        name="pack",
    )(counts, f_start.reshape(1, states), coef)


def merge_logs(parts):
    highest = jnp.max(parts, axis=0)
    return highest + jnp.log2(jnp.sum(jnp.exp2(parts - highest[None]), axis=0))


def merge_kernel(parts_ref, out_ref):
    out_ref[...] = jnp.broadcast_to(merge_logs(parts_ref[...])[None], out_ref.shape)


def merge(parts, copies):
    return pl.pallas_call(
        merge_kernel,
        out_shape=jax.ShapeDtypeStruct((copies,) + parts.shape[1:], jnp.float32),
        name="merge",
    )(parts)


def centered(value):
    mean = jnp.sum(jnp.sum(value, axis=1, keepdims=True), axis=0, keepdims=True) / value.size
    return value - mean


def sweep_kernel(
    first,
    group_ref,
    packed_ref,
    energy_ref,
    anchor_ref,
    *rest,
):
    if first:
        part_ref, wide_ref, column_ref, left_ref, right_ref, weight_ref, scaled_ref, high_ref, norm_ref, acc_ref, top_ref = rest
    else:
        parts_ref, old_ref, part_ref, wide_ref, column_ref, left_ref, right_ref, weight_ref, scaled_ref, high_ref, norm_ref, acc_ref, top_ref = rest
    groups = packed_ref.shape[0]
    components = energy_ref.shape[0]
    samples = energy_ref.shape[1]
    states = groups * STATE_TILE
    pair = STATE_TILE // LANES

    for g in range(groups):
        rows = packed_ref[g, components:, :].astype(jnp.float32)
        log_counts = rows[0:1] + rows[1:2] + rows[2:3]
        start = rows[3:4] + rows[4:5] + rows[5:6]
        for h in range(pair):
            at = pair * g + h
            lanes = slice(h * LANES, (h + 1) * LANES)
            column_ref[at : at + 1, :] = log_counts[:, lanes]
            if first:
                wide_ref[at : at + 1, :] = log_counts[:, lanes] + start[:, lanes]
    if not first:
        raw = old_ref[...] - merge_logs(parts_ref[...]) * LN2
        wide_ref[...] = column_ref[...] + centered(raw)

    for g in range(groups):
        coef = packed_ref[g, :components, :].astype(jnp.float32) * (-LOG2E)
        both = [wide_ref[pair * g + h : pair * g + h + 1, :] for h in range(pair)]
        weight = jnp.concatenate(both, axis=1) * LOG2E
        w0, w1, w2 = split3(weight)
        row = lax.broadcasted_iota(jnp.int32, (DEPTH - 3 * components, STATE_TILE), 0)
        tail = jnp.where(row == 0, w0, jnp.where(row == 1, w1, jnp.where(row == 2, w2, 0.0)))
        block = jnp.concatenate(list(split3(coef)) + [tail], axis=0)
        left_ref[g * STATE_TILE : (g + 1) * STATE_TILE, :] = block.T.astype(jnp.bfloat16)
    for k in range(3):
        right_ref[k * components : (k + 1) * components, :] = energy_ref[...]
    row = lax.broadcasted_iota(jnp.int32, (DEPTH - 3 * components, samples), 0)
    right_ref[3 * components :, :] = jnp.where(row < 3, 1.0, 0.0).astype(jnp.bfloat16)

    live = anchor_ref[...] < states
    weight_ref[...] = jnp.where(live, 1.0, 0.0)

    def scores(g, tile):
        return lax.dot_general(
            left_ref[g * STATE_TILE : (g + 1) * STATE_TILE, :] if isinstance(g, int) else left_ref[pl.ds(pl.multiple_of(g * STATE_TILE, STATE_TILE), STATE_TILE), :],
            right_ref[:, tile],
            (((1,), (0,)), ((), ())),
            preferred_element_type=jnp.float32,
        )

    tiles = samples // SAMPLE_TILE
    for t in range(tiles):
        tile = slice(t * SAMPLE_TILE, (t + 1) * SAMPLE_TILE)
        high = jnp.full((1, SAMPLE_TILE), LOW, jnp.float32)
        total = jnp.zeros((1, SAMPLE_TILE), jnp.float32)
        for g in range(groups):
            score = scores(g, tile)
            newer = jnp.maximum(high, jnp.max(score, axis=0, keepdims=True))
            scaled = jnp.exp2(score - newer)
            scaled_ref[g * STATE_TILE : (g + 1) * STATE_TILE, :] = scaled
            total = total * jnp.exp2(high - newer) + jnp.sum(scaled, axis=0, keepdims=True)
            high = newer
            high_ref[g : g + 1, :] = high
        norm_ref[:, tile] = high + jnp.log2(total)
        share = weight_ref[:, tile] / total
        for g in range(groups):
            factor = share * jnp.exp2(high_ref[g : g + 1, :] - high)
            part = scaled_ref[g * STATE_TILE : (g + 1) * STATE_TILE, :] * factor
            folded = part[:, :LANES]
            for k in range(1, SAMPLE_TILE // LANES):
                folded += part[:, k * LANES : (k + 1) * LANES]
            rows = slice(g * STATE_TILE, (g + 1) * STATE_TILE)
            if t == 0:
                acc_ref[rows, :] = folded
            else:
                acc_ref[rows, :] += folded

    diagonal = lax.broadcasted_iota(jnp.int32, (LANES, LANES), 0) == lax.broadcasted_iota(
        jnp.int32, (LANES, LANES), 1
    )

    def to_lanes(column):
        return jnp.sum(jnp.where(diagonal, column, 0.0), axis=0, keepdims=True)

    for k in range(states // LANES):
        rows = slice(k * LANES, (k + 1) * LANES)
        column_ref[k : k + 1, :] = to_lanes(jnp.sum(acc_ref[rows, :], axis=1, keepdims=True))
    sums = column_ref[...]
    some_live = jnp.max(weight_ref[...]) > 0.0
    result = jnp.where(sums > 0.0, jnp.log2(jnp.maximum(sums, SAFE_SUM)), LOW)
    part_ref[...] = jnp.broadcast_to(result[None], part_ref.shape)

    @pl.when(jnp.logical_and(some_live, jnp.min(sums) < SAFE_SUM))
    def exact():
        acc_ref[...] = jnp.zeros_like(acc_ref)
        top_ref[...] = jnp.full_like(top_ref, LOW)

        def visit(step, carry):
            g = step // (samples // LANES)
            at = pl.multiple_of((step % (samples // LANES)) * LANES, LANES)
            tile = pl.ds(at, LANES)
            rows = pl.ds(pl.multiple_of(g * STATE_TILE, STATE_TILE), STATE_TILE)
            is_live = weight_ref[:, tile] > 0.0
            term = jnp.where(is_live, scores(g, tile) - norm_ref[:, tile], LOW)
            older = top_ref[rows, :]
            newer = jnp.maximum(older, term)
            added = jnp.where(is_live, jnp.exp2(term - newer), 0.0)
            acc_ref[rows, :] = acc_ref[rows, :] * jnp.exp2(older - newer) + added
            top_ref[rows, :] = newer
            return carry

        lax.fori_loop(0, groups * (samples // LANES), visit, 0)
        for k in range(states // LANES):
            rows = slice(k * LANES, (k + 1) * LANES)
            top = jnp.max(top_ref[rows, :], axis=1, keepdims=True)
            total = jnp.sum(acc_ref[rows, :] * jnp.exp2(top_ref[rows, :] - top), axis=1, keepdims=True)
            value = to_lanes(top + jnp.log2(total))
            part_ref[:, k : k + 1, :] = jnp.broadcast_to(value[None], (part_ref.shape[0], 1, LANES))


def sweep(group, packed, energy, anchor, parts, old, copies):
    groups, packed_rows, _ = packed.shape
    components, columns = energy.shape
    states = groups * STATE_TILE
    share = columns // groups
    first = parts is None
    tall = states // LANES
    operands = [packed, energy, anchor.reshape(1, columns)]
    in_specs = [
        pl.BlockSpec(packed.shape, lambda i, g: (0, 0, 0)),
        pl.BlockSpec((components, share), lambda i, g: (0, g[0])),
        pl.BlockSpec((1, share), lambda i, g: (0, g[0])),
    ]
    if not first:
        operands += [parts, old]
        in_specs += [
            pl.BlockSpec(parts.shape, lambda i, g: (0, 0, 0)),
            pl.BlockSpec(old.shape, lambda i, g: (0, 0)),
        ]
    return pl.pallas_call(
        functools.partial(sweep_kernel, first),
        out_shape=[
            jax.ShapeDtypeStruct((copies, tall, LANES), jnp.float32),
            jax.ShapeDtypeStruct((tall, LANES), jnp.float32),
        ],
        grid_spec=pltpu.PrefetchScalarGridSpec(
            num_scalar_prefetch=1,
            grid=(1,),
            in_specs=in_specs,
            out_specs=[
                pl.BlockSpec((copies, tall, LANES), lambda i, g: (0, 0, 0)),
                pl.BlockSpec((tall, LANES), lambda i, g: (0, 0)),
            ],
            scratch_shapes=[
                pltpu.VMEM((tall, LANES), jnp.float32),
                pltpu.VMEM((states, DEPTH), jnp.bfloat16),
                pltpu.VMEM((DEPTH, share), jnp.bfloat16),
                pltpu.VMEM((1, share), jnp.float32),
                pltpu.VMEM((states, SAMPLE_TILE), jnp.float32),
                pltpu.VMEM((groups, SAMPLE_TILE), jnp.float32),
                pltpu.VMEM((1, share), jnp.float32),
                pltpu.VMEM((states, LANES), jnp.float32),
                pltpu.VMEM((states, LANES), jnp.float32),
            ],
        ),
        compiler_params=pltpu.CompilerParams(vmem_limit_bytes=40 * 2**20),
        name="sweep",
    )(group, *operands)


def finish_kernel(group_ref, parts_ref, old_ref, out_ref, hold_ref):
    raw = old_ref[...] - merge_logs(parts_ref[...]) * LN2
    hold_ref[...] = centered(raw)
    out_ref[...] = hold_ref[pl.ds(group_ref[0] * out_ref.shape[0], out_ref.shape[0]), :]


def finish(group, parts, old):
    rows = old.shape[0] // parts.shape[0]
    return pl.pallas_call(
        finish_kernel,
        out_shape=jax.ShapeDtypeStruct((rows, LANES), jnp.float32),
        grid_spec=pltpu.PrefetchScalarGridSpec(
            num_scalar_prefetch=1,
            grid=(1,),
            in_specs=[
                pl.BlockSpec(parts.shape, lambda i, g: (0, 0, 0)),
                pl.BlockSpec(old.shape, lambda i, g: (0, 0)),
            ],
            out_specs=pl.BlockSpec((rows, LANES), lambda i, g: (0, 0)),
            scratch_shapes=[pltpu.VMEM(old.shape, jnp.float32)],
        ),
        name="finish",
    )(group, parts, old)


def spread(copies, axis):
    return lax.all_to_all(copies, axis, 0, 0)


def per_device(energy, coef, anchor, f_start):
    groups = lax.axis_size("state")
    blocks = lax.axis_size("sample")
    group = lax.axis_index("state").astype(jnp.int32).reshape(1)
    counts = spread(histogram(group, anchor, blocks), "sample")
    packed = spread(pack(counts, f_start, coef, groups), "state")
    parts = None
    weights = None
    for iteration in range(ITERS):
        part, weights = sweep(group, packed, energy, anchor, parts, weights, blocks)
        parts = spread(merge(spread(part, "sample"), groups), "state")
    return finish(group, parts, weights).reshape(-1)


def solution(mesh):
    in_specs = (P(None, "sample"), P(None, "state"), P("sample"), P("state"))
    out_specs = P("state")
    return jax.shard_map(
        per_device, mesh=mesh, in_specs=in_specs, out_specs=out_specs, check_vma=False
    )
```

time: 798 us -> 132 us (0.17); the launches traced: 789 us -> 131 us
  other arithmetic: 255 us -> 0 us
  waiting for transfers between devices: 203 us -> 0 us
  blocking collectives: 170 us -> 90.2 us
  matrix products: 75.3 us -> 0 us
  local copies, waits for them, and re-layouts: 66.3 us -> 3.09 us
  Pallas kernels: 0 us -> 37.8 us
  between operations: 16 us -> 0.04 us
    scatter-add x1 -> x0, other arithmetic: 204 us -> none  [per_device(): jax.ops.segment_sum(jnp.ones(anchor.shape, jnp.float32), anchor, num_segm...]
    all_gather x4 -> x0, waiting for transfers between devices: 202 us -> none  [merged(): everything = jax.tree.map(lambda part: lax.all_gather(part, axis), value)]
    psum x3 -> x0, blocking collectives: 103 us -> none  [the longest x2 63.2 us: center(): summed = lax.psum(jnp.sum(unshifted), 'state')]
    all_to_all x0 -> x6, blocking collectives: none -> 90.2 us  [spread(): return lax.all_to_all(copies, axis, 0, 0)]
    dot_general x32 -> x0, matrix products: 75.3 us -> none  [potentials(): lax.dot_general(coef_part, tile_data, (((0,), (0,)), ((), ())), preferred...]
    all_gather x4 -> x0, blocking collectives: 67.5 us -> none  [merged(): everything = jax.tree.map(lambda part: lax.all_gather(part, axis), value)]
    reduce_sum x34 -> x0, other arithmetic: 45.2 us -> none  [the longest x16 34.5 us: row_terms(): jnp.sum(jnp.where(live_part[None, :], jnp.exp(weighted - highest[:, None]...]
    dynamic_slice x93 -> x0, local copies, waits for them, and re-layouts: 43.1 us -> none  [the longest x60 42.7 us: turn(): return combine(so_far, jax.tree.map(lambda part: part[k], everything))]
  transfers between devices with their start and end apart: 4 -> 0, of which waited for: 4 -> 0; matrix products, arithmetic and copies ran while one was open for 0% -> 0% of each run, Pallas kernels for 0% -> 0%
where the time goes in v1:
time: 132 us; the launch traced here: 131 us
  blocking collectives  90.2 us (68%)
  Pallas kernels  37.8 us (29%)
  local copies, waits for them, and re-layouts  3.09 us (2%)
    all_to_all x6, blocking collectives, spread(): return lax.all_to_all(copies, axis, 0, 0)  90.2 us
    pallas_call x2, Pallas kernels, sweep(): pl.pallas_call(functools.partial(sweep_kernel, first), out_shape=[jax.Sha...  28.8 us
    pallas_call x2, Pallas kernels, merge(): pl.pallas_call(merge_kernel, out_shape=jax.ShapeDtypeStruct((copies,) + p...  3.45 us
    unnamed x10, local copies, waits for them, and re-layouts  3.09 us

profile of v1, /device:TPU:1, one launch (start us, length us, event | category | flops | bytes accessed | tf_op | source)
XLA Modules:
  0.0 131.1 jit_solution(11155655017273382887)
XLA Ops:
  0.0 2.3 %histogram.1 = f32[16,1,256]{2,1,0:T(1,128)} custom-call(s32[1]{0:T(128)} %bitcast.group_ref, s32[1,32768]{1,0:T(1,128)} %bitcast.4), custom_call_target="tpu_custom_call" | custom-call | tf_op jit(solution)/shard_map/histogram/pallas_call | solution.py:62
  2.3 17.4 %all_to_all.30.counts_ref = f32[16,1,256]{2,1,0:T(1,128)} all-to-all(f32[16,1,256]{2,1,0:T(1,128)} %histogram.1), channel_id=1, replica_groups=mesh['state'=16,'sample'=16] {'sample'}, dimensions={0} | all-to-all | bytes 32768 | tf_op jit(solution)/shard_map/all_to_all | solution.py:318
  19.7 1.5 %pack.1 = bf16[16,40,256]{2,1,0:T(8,128)(2,1)} custom-call(f32[16,1,256]{2,1,0:T(1,128)} %all_to_all.30.counts_ref, f32[1,256]{1,0:T(1,128)} %bitcast.7, bf16[32,256]{1,0:T(8,128)(2,1)} %coef_ref.1), custom_call_target="tpu_custom_call" | custom-call | tf_op jit(solution)/shard_map/pack/pallas_call | solution.py:86
  21.3 14.7 %all_to_all.31.packed_ref = bf16[16,40,256]{2,1,0:T(8,128)(2,1)S(1)} all-to-all(bf16[16,40,256]{2,1,0:T(8,128)(2,1)} %pack.1), channel_id=1, replica_groups=mesh['state'=16,'sample'=16] {'state'}, dimensions={0} | all-to-all | bytes 655360 | tf_op jit(solution)/shard_map/all_to_all | solution.py:318
  36.0 0.0 copy-start
  36.0 1.6 %copy-done = bf16[32,32768]{1,0:T(8,128)(2,1)S(1)} copy-done((bf16[32,32768]{1,0:T(8,128)(2,1)S(1)}, bf16[32,32768]{1,0:T(8,128)(2,1)}, u32[]{:S(2)}) %copy-start) | copy-done | bytes 2097176
  37.6 0.0 copy-start.2
  37.6 0.9 copy-done.2
  38.5 0.0 copy-start.1
  38.5 0.0 copy-start.3
  38.5 14.4 %sweep.2 = (f32[16,32,128]{2,1,0:T(8,128)S(1)}, f32[32,128]{1,0:T(8,128)S(1)}) custom-call(s32[1]{0:T(128)} %bitcast.group_ref, bf16[16,40,256]{2,1,0:T(8,128)(2,1)S(1)} %all_to_all.31.packed_ref, bf16[32,32768]{1,0:T(8,128)(2,1)S(1)} %copy-done, s32[1,32768]{1,0:T(1,128)S(1)} %bitcast.5), custom_call_target="tpu_custom_call" | custom-call | tf_op jit(solution)/shard_map/sweep/pallas_call | solution.py:261
  52.9 17.2 %all_to_all.32.parts_ref = f32[16,32,128]{2,1,0:T(8,128)} all-to-all(f32[16,32,128]{2,1,0:T(8,128)S(1)} %get-tuple-element.9), channel_id=1, replica_groups=mesh['state'=16,'sample'=16] {'sample'}, dimensions={0} | all-to-all | bytes 524288 | tf_op jit(solution)/shard_map/all_to_all | solution.py:318
  70.1 1.7 %merge.2 = f32[16,32,128]{2,1,0:T(8,128)} custom-call(f32[16,32,128]{2,1,0:T(8,128)} %all_to_all.32.parts_ref), custom_call_target="tpu_custom_call" | custom-call | tf_op jit(solution)/shard_map/merge/pallas_call | solution.py:103
  71.8 12.7 %all_to_all.33.rest_0_ = f32[16,32,128]{2,1,0:T(8,128)S(1)} all-to-all(f32[16,32,128]{2,1,0:T(8,128)} %merge.2), channel_id=1, replica_groups=mesh['state'=16,'sample'=16] {'state'}, dimensions={0} | all-to-all | bytes 524288 | tf_op jit(solution)/shard_map/all_to_all | solution.py:318
  84.5 0.0 copy-done.1
  84.5 0.0 copy-done.3
  84.5 14.4 %sweep.3 = (f32[16,32,128]{2,1,0:T(8,128)S(1)}, f32[32,128]{1,0:T(8,128)S(1)}) custom-call(s32[1]{0:T(128)} %bitcast.group_ref, bf16[16,40,256]{2,1,0:T(8,128)(2,1)S(1)} %all_to_all.31.packed_ref, bf16[32,32768]{1,0:T(8,128)(2,1)S(1)} %copy-done.1, s32[1,32768]{1,0:T(1,128)S(1)} %bitcast.6, f32[16,32,128]{2,1,0:T(8,128)S(1)} %all_to_all.33.rest_0_, ...), custom_call_target="tpu_custom_call" | custom-call | tf_op jit(solution)/shard_map/sweep/pallas_call | solution.py:261
  98.9 0.0 copy-start.4
  98.9 0.6 copy-done.4
  99.5 15.4 %all_to_all.34.parts_ref = f32[16,32,128]{2,1,0:T(8,128)} all-to-all(f32[16,32,128]{2,1,0:T(8,128)S(1)} %get-tuple-element.11), channel_id=1, replica_groups=mesh['state'=16,'sample'=16] {'sample'}, dimensions={0} | all-to-all | bytes 524288 | tf_op jit(solution)/shard_map/all_to_all | solution.py:318
  114.9 1.7 %merge.3 = f32[16,32,128]{2,1,0:T(8,128)} custom-call(f32[16,32,128]{2,1,0:T(8,128)} %all_to_all.34.parts_ref), custom_call_target="tpu_custom_call" | custom-call | tf_op jit(solution)/shard_map/merge/pallas_call | solution.py:103
  116.6 12.8 %all_to_all.35.parts_ref = f32[16,32,128]{2,1,0:T(8,128)} all-to-all(f32[16,32,128]{2,1,0:T(8,128)} %merge.3), channel_id=1, replica_groups=mesh['state'=16,'sample'=16] {'state'}, dimensions={0} | all-to-all | bytes 524288 | tf_op jit(solution)/shard_map/all_to_all | solution.py:318
  129.5 1.7 %finish.1 = f32[2,128]{1,0:T(2,128)} custom-call(s32[1]{0:T(128)} %bitcast.group_ref, f32[16,32,128]{2,1,0:T(8,128)} %all_to_all.35.parts_ref, f32[32,128]{1,0:T(8,128)} %copy-done.4), custom_call_target="tpu_custom_call" | custom-call | tf_op jit(solution)/shard_map/finish/pallas_call | solution.py:300
Async XLA Ops:
  36.0 1.6 %copy-start = (bf16[32,32768]{1,0:T(8,128)(2,1)S(1)}, bf16[32,32768]{1,0:T(8,128)(2,1)}, u32[]{:S(2)}) copy-start(bf16[32,32768]{1,0:T(8,128)(2,1)} %energy_ref.3) | copy-start | bytes 6291460
  37.6 0.9 copy-start.2
  38.5 46.0 %copy-start.1 = (bf16[32,32768]{1,0:T(8,128)(2,1)S(1)}, bf16[32,32768]{1,0:T(8,128)(2,1)}, u32[]{:S(2)}) copy-start(bf16[32,32768]{1,0:T(8,128)(2,1)} %energy_ref.3) | copy-start | bytes 6291460
  38.5 46.0 %copy-start.3 = (s32[32768]{0:T(1024)S(1)}, s32[32768]{0:T(1024)}, u32[]{:S(2)}) copy-start(s32[32768]{0:T(1024)} %param.6) | copy-start | bytes 393220
  98.9 0.6 copy-start.4

commit v2 on v1

v2 whole, which is shorter than its diff:
```python
import functools

import jax
import jax.numpy as jnp
from jax import lax
from jax.experimental import pallas as pl
from jax.experimental.pallas import tpu as pltpu
from jax.sharding import PartitionSpec as P

ITERS = 2

LOG2E = 1.4426950408889634
LN2 = 0.6931471805599453
LOW = -1.0e30
SAFE_SUM = 1.0e-25
SAFE_TOP = 1.0e30

LANES = 128
STATE_TILE = 256
ROW_TILE = 512
DEPTH = 128
WEIGHT_AT = 96
SHIFT_AT = 99
LIVE_AT = 102


def split3(value):
    high = value.astype(jnp.bfloat16).astype(jnp.float32)
    rest = value - high
    middle = rest.astype(jnp.bfloat16).astype(jnp.float32)
    low = (rest - middle).astype(jnp.bfloat16).astype(jnp.float32)
    return high, middle, low


def prepare_kernel(group_ref, anchor_ref, own_ref, energy_ref, out_ref, left_ref):
    base = group_ref[0] * 16
    total = anchor_ref.shape[1]
    step = 4096
    row = lax.broadcasted_iota(jnp.int32, (16, step), 0)
    counts = jnp.zeros((16, 16), jnp.float32)
    for start in range(0, total, step):
        anchor = anchor_ref[:, start : start + step]
        high = lax.shift_right_logical(anchor, 4) - base
        low = lax.bitwise_and(anchor, 15)
        high_hot = jnp.where(row == high, 1.0, 0.0).astype(jnp.bfloat16)
        low_hot = jnp.where(row == low, 1.0, 0.0).astype(jnp.bfloat16)
        counts += lax.dot_general(
            high_hot, low_hot, (((1,), (1,)), ((), ())), preferred_element_type=jnp.float32
        )
    lane = lax.broadcasted_iota(jnp.int32, (16, 256), 1)
    row16 = lax.broadcasted_iota(jnp.int32, (16, 256), 0)
    spread_out = jnp.where(lax.bitwise_and(lane, 15) == row16, 1.0, 0.0)
    placed = lax.dot_general(
        counts,
        spread_out,
        (((1,), (0,)), ((), ())),
        preferred_element_type=jnp.float32,
        precision=lax.Precision.HIGHEST,
    )
    flat = jnp.sum(jnp.where(lax.shift_right_logical(lane, 4) == row16, placed, 0.0), axis=0, keepdims=True)
    out_ref[...] = jnp.broadcast_to(flat[None], out_ref.shape)

    components, samples = energy_ref.shape
    live = jnp.where(own_ref[...] < 16 * 256, 1.0, 0.0)
    energy = energy_ref[...].astype(jnp.float32) * live
    row = lax.broadcasted_iota(jnp.int32, (DEPTH - 3 * components, samples), 0)
    ones = row < SHIFT_AT - WEIGHT_AT
    tail = jnp.where(ones, 1.0, jnp.where(row == LIVE_AT - WEIGHT_AT, live, 0.0))
    block = jnp.concatenate([energy, energy, energy, tail], axis=0)
    for at in range(0, samples, 256):
        left_ref[at : at + 256, :] = block[:, at : at + 256].T.astype(jnp.bfloat16)


def prepare(group, anchor, energy, copies, groups):
    total = anchor.shape[0]
    components = energy.shape[0]
    share = total // groups
    row = anchor.reshape(1, total)
    return pl.pallas_call(
        prepare_kernel,
        out_shape=[
            jax.ShapeDtypeStruct((copies, 1, 256), jnp.float32),
            jax.ShapeDtypeStruct((share, DEPTH), jnp.bfloat16),
        ],
        grid_spec=pltpu.PrefetchScalarGridSpec(
            num_scalar_prefetch=1,
            grid=(1,),
            in_specs=[
                pl.BlockSpec((1, total), lambda i, g: (0, 0)),
                pl.BlockSpec((1, share), lambda i, g: (0, g[0])),
                pl.BlockSpec((components, share), lambda i, g: (0, g[0])),
            ],
            out_specs=[
                pl.BlockSpec((copies, 1, 256), lambda i, g: (0, 0, 0)),
                pl.BlockSpec((share, DEPTH), lambda i, g: (0, 0)),
            ],
        ),
        name="prepare",
    )(group, row, row, energy)


def pack_kernel(counts_ref, start_ref, coef_ref, out_ref):
    counts = jnp.sum(counts_ref[...], axis=0)
    log_counts = jnp.log(counts)
    rows = list(split3(log_counts)) + list(split3(start_ref[...]))
    rows.append(jnp.zeros((2,) + counts.shape[1:], jnp.float32))
    packed = jnp.concatenate([coef_ref[...].astype(jnp.float32)] + rows, axis=0).astype(jnp.bfloat16)
    out_ref[...] = jnp.broadcast_to(packed[None], out_ref.shape)


def pack(counts, f_start, coef, copies):
    components, states = coef.shape
    return pl.pallas_call(
        pack_kernel,
        out_shape=jax.ShapeDtypeStruct((copies, components + 8, states), jnp.bfloat16),
        name="pack",
    )(counts, f_start.reshape(1, states), coef)


def merge_logs(parts):
    highest = jnp.max(parts, axis=0)
    return highest + jnp.log2(jnp.sum(jnp.exp2(parts - highest[None]), axis=0))


def merge_kernel(parts_ref, out_ref):
    out_ref[...] = jnp.broadcast_to(merge_logs(parts_ref[...])[None], out_ref.shape)


def merge(parts, copies):
    return pl.pallas_call(
        merge_kernel,
        out_shape=jax.ShapeDtypeStruct((copies,) + parts.shape[1:], jnp.float32),
        name="merge",
    )(parts)


def centered(value):
    mean = jnp.sum(jnp.sum(value, axis=1, keepdims=True), axis=0, keepdims=True) / value.size
    return value - mean


def largest(value):
    return jnp.max(jnp.max(value, axis=1, keepdims=True), axis=0, keepdims=True)


def folded(value, combine):
    return combine(value[:, :LANES], value[:, LANES:])


def sweep_kernel(first, *refs):
    if first:
        packed_ref, left_ref, part_ref, wide_ref, shifted_ref, right_ref, scaled_ref, acc_ref, some_ref, norm_ref, top_ref = refs
        source_ref = shifted_ref
    else:
        packed_ref, left_ref, parts_ref, old_ref, part_ref, wide_ref, some_ref, right_ref, scaled_ref, acc_ref, norm_ref, top_ref = refs
        source_ref = left_ref
    groups, packed_rows, _ = packed_ref.shape
    components = packed_rows - 8
    samples = left_ref.shape[0]
    states = groups * STATE_TILE
    pair = STATE_TILE // LANES
    tiles = samples // ROW_TILE

    for g in range(groups):
        rows = packed_ref[g, components:, :].astype(jnp.float32)
        log_counts = rows[0:1] + rows[1:2] + rows[2:3]
        value = log_counts + (rows[3:4] + rows[4:5] + rows[5:6]) if first else log_counts
        for h in range(pair):
            wide_ref[pair * g + h : pair * g + h + 1, :] = value[:, h * LANES : (h + 1) * LANES]
    if first:
        weights = wide_ref[...]
    else:
        raw = old_ref[...] - merge_logs(parts_ref[...]) * LN2
        wide = wide_ref[...] + centered(raw)
        wide_ref[...] = wide
        weights = wide - largest(wide - old_ref[...])
    w0, w1, w2 = split3(weights * LOG2E)

    row = lax.broadcasted_iota(jnp.int32, (DEPTH - 3 * components, LANES), 0)
    ones = jnp.where(row < LIVE_AT - WEIGHT_AT, 1.0, 0.0)
    for g in range(groups):
        coef = packed_ref[g, :components, :].astype(jnp.float32) * (-LOG2E)
        lanes = slice(g * STATE_TILE, (g + 1) * STATE_TILE)
        for k, part in enumerate(split3(coef)):
            right_ref[k * components : (k + 1) * components, lanes] = part.astype(jnp.bfloat16)
        for h in range(pair):
            at = pair * g + h
            tail = jnp.where(row == 0, w0[at : at + 1], jnp.where(row == 1, w1[at : at + 1], jnp.where(row == 2, w2[at : at + 1], ones)))
            right_ref[WEIGHT_AT:, at * LANES : (at + 1) * LANES] = tail.astype(jnp.bfloat16)

    def product(left, right):
        return lax.dot_general(left, right, (((1,), (0,)), ((), ())), preferred_element_type=jnp.float32)

    if first:
        lane = lax.broadcasted_iota(jnp.int32, (DEPTH, LANES), 1)
        for h in range(2):
            some = jnp.zeros((DEPTH, LANES), jnp.float32)
            for j in range(8):
                g = 8 * h + j
                tile = right_ref[:, g * STATE_TILE : g * STATE_TILE + LANES].astype(jnp.float32)
                moved = tile if j == 0 else pltpu.roll(tile, 16 * j, 1)
                some = jnp.where(lax.shift_right_logical(lane, 4) == j, moved, some)
            some_ref[:, h * LANES : (h + 1) * LANES] = some.astype(jnp.bfloat16)

    acc_ref[...] = jnp.zeros_like(acc_ref)
    lane = lax.broadcasted_iota(jnp.int32, (ROW_TILE, LANES), 1)

    def shifted(block, shift):
        s0, s1, s2 = split3(-shift)
        values = jnp.where(lane == SHIFT_AT, s0, jnp.where(lane == SHIFT_AT + 1, s1, s2))
        chosen = jnp.logical_and(lane >= SHIFT_AT, lane < LIVE_AT)
        return jnp.where(chosen, values, block.astype(jnp.float32)).astype(jnp.bfloat16)

    def visit(t, carry):
        least, most = carry
        rows = pl.ds(pl.multiple_of(t * ROW_TILE, ROW_TILE), ROW_TILE)
        left = left_ref[rows, :]
        if first:
            sampled = folded(product(left, some_ref[...]), jnp.maximum)
            shift = jnp.max(sampled, axis=1, keepdims=True)
            left = shifted(left, shift)
        live = left_ref[rows, LIVE_AT : LIVE_AT + 1].astype(jnp.float32)
        total = jnp.zeros((ROW_TILE, LANES), jnp.float32)
        for g in range(groups):
            lanes = slice(g * STATE_TILE, (g + 1) * STATE_TILE)
            scaled = jnp.exp2(product(left, right_ref[:, lanes]))
            scaled_ref[:, lanes] = scaled
            total += folded(scaled, jnp.add)
        denominator = jnp.sum(total, axis=1, keepdims=True)
        least = jnp.minimum(least, jnp.where(live > 0.0, denominator, 1.0))
        most = jnp.maximum(most, jnp.where(live > 0.0, denominator, 1.0))
        share = jnp.broadcast_to(live / denominator, (ROW_TILE, LANES))
        if first:
            shifted_ref[rows, :] = shifted(left, shift + jnp.log2(denominator))
        for k in range(states // LANES):
            lanes = slice(k * LANES, (k + 1) * LANES)
            part = scaled_ref[:, lanes] * share
            acc_ref[:, lanes] += jnp.sum(part.reshape(ROW_TILE // 8, 8, LANES), axis=0)
        return least, most

    unit = jnp.ones((ROW_TILE, 1), jnp.float32)
    least, most = lax.fori_loop(0, tiles, visit, (unit, unit))
    least = jnp.min(least)
    most = jnp.max(most)
    sums = jnp.sum(acc_ref[...], axis=0, keepdims=True)
    smallest = jnp.min(sums)
    some_live = jnp.max(left_ref[:, LIVE_AT : LIVE_AT + 1].astype(jnp.float32)) > 0.0
    logs = jnp.where(sums > 0.0, jnp.log2(jnp.maximum(sums, SAFE_SUM)), LOW)

    def give(value):
        for k in range(states // LANES):
            piece = value[:, k * LANES : (k + 1) * LANES]
            part_ref[:, k : k + 1, :] = jnp.broadcast_to(piece[None], (part_ref.shape[0], 1, LANES))

    give(logs)
    enough = jnp.logical_and(smallest >= SAFE_SUM, smallest * least >= SAFE_SUM)
    safe = jnp.logical_and(enough, jnp.logical_and(most < SAFE_TOP, least > SAFE_SUM))

    @pl.when(jnp.logical_and(some_live, jnp.logical_not(safe)))
    def exact():
        acc_ref[...] = jnp.zeros_like(acc_ref)
        top_ref[...] = jnp.full_like(top_ref, LOW)

        def tile_at(k):
            return pl.ds(pl.multiple_of(k * LANES, LANES), LANES)

        def slots(t, carry):
            rows = pl.ds(pl.multiple_of(t * ROW_TILE, ROW_TILE), ROW_TILE)
            left = left_ref[rows, :]
            is_live = jnp.broadcast_to(left[:, LIVE_AT : LIVE_AT + 1].astype(jnp.float32), (ROW_TILE, LANES)) > 0.0

            def column(k, pieces):
                high, total = pieces
                score = product(left, right_ref[:, tile_at(k)])
                newer = jnp.maximum(high, score)
                return newer, total * jnp.exp2(high - newer) + jnp.exp2(score - newer)

            start = (jnp.full((ROW_TILE, LANES), LOW, jnp.float32), jnp.zeros((ROW_TILE, LANES), jnp.float32))
            high, total = lax.fori_loop(0, states // LANES, column, start)
            top = jnp.max(high, axis=1, keepdims=True)
            total = jnp.sum(total * jnp.exp2(high - top), axis=1, keepdims=True)
            norm = top + jnp.log2(total)
            if first:
                shifted_ref[rows, :] = shifted(left, norm)

            def state(k, inner):
                lanes = tile_at(k)
                term = jnp.where(is_live, product(left, right_ref[:, lanes]) - norm, LOW)
                older = top_ref[:, lanes]
                newer = jnp.maximum(older, jnp.max(term, axis=0, keepdims=True))
                added = jnp.sum(jnp.where(is_live, jnp.exp2(term - newer), 0.0), axis=0, keepdims=True)
                acc_ref[0:1, lanes] = acc_ref[0:1, lanes] * jnp.exp2(older - newer) + added
                top_ref[:, lanes] = newer
                return inner

            return lax.fori_loop(0, states // LANES, state, carry)

        lax.fori_loop(0, tiles, slots, 0)
        give(top_ref[...] + jnp.log2(acc_ref[0:1, :]))


def whole(shape):
    return pl.BlockSpec(shape, lambda: (0,) * len(shape))


def sweep(packed, left, parts, old, copies):
    groups = packed.shape[0]
    states = groups * STATE_TILE
    samples = left.shape[0]
    first = parts is None
    tall = states // LANES
    operands = [packed, left] + ([] if first else [parts, old])
    outs = [((copies, tall, LANES), jnp.float32), ((tall, LANES), jnp.float32)]
    scratch = [
        pltpu.VMEM((DEPTH, states), jnp.bfloat16),
        pltpu.VMEM((ROW_TILE, states), jnp.float32),
        pltpu.VMEM((8, states), jnp.float32),
        pltpu.VMEM((DEPTH, 2 * LANES), jnp.bfloat16),
        pltpu.VMEM((8, LANES), jnp.float32),
        pltpu.VMEM((1, states), jnp.float32),
    ]
    if first:
        outs.append((left.shape, jnp.bfloat16))
    else:
        scratch = [scratch[3]] + scratch[:3] + scratch[4:]
    return pl.pallas_call(
        functools.partial(sweep_kernel, first),
        out_shape=[jax.ShapeDtypeStruct(*out) for out in outs],
        scratch_shapes=scratch,
        compiler_params=pltpu.CompilerParams(vmem_limit_bytes=40 * 2**20),
        name="first_sweep" if first else "next_sweep",
    )(*operands)


def finish_kernel(group_ref, parts_ref, old_ref, out_ref, hold_ref):
    raw = old_ref[...] - merge_logs(parts_ref[...]) * LN2
    hold_ref[...] = centered(raw)
    out_ref[...] = hold_ref[pl.ds(group_ref[0] * out_ref.shape[0], out_ref.shape[0]), :]


def finish(group, parts, old):
    rows = old.shape[0] // parts.shape[0]
    return pl.pallas_call(
        finish_kernel,
        out_shape=jax.ShapeDtypeStruct((rows, LANES), jnp.float32),
        grid_spec=pltpu.PrefetchScalarGridSpec(
            num_scalar_prefetch=1,
            grid=(1,),
            in_specs=[
                pl.BlockSpec(parts.shape, lambda i, g: (0, 0, 0)),
                pl.BlockSpec(old.shape, lambda i, g: (0, 0)),
            ],
            out_specs=pl.BlockSpec((rows, LANES), lambda i, g: (0, 0)),
            scratch_shapes=[pltpu.VMEM(old.shape, jnp.float32)],
        ),
        name="finish",
    )(group, parts, old)


def spread(copies, axis):
    return lax.all_to_all(copies, axis, 0, 0)


def per_device(energy, coef, anchor, f_start):
    groups = lax.axis_size("state")
    blocks = lax.axis_size("sample")
    group = lax.axis_index("state").astype(jnp.int32).reshape(1)
    counts, left = prepare(group, anchor, energy, blocks, groups)
    counts = spread(counts, "sample")
    packed = spread(pack(counts, f_start, coef, groups), "state")
    parts = None
    weights = None
    for iteration in range(ITERS):
        part, weights, *rest = sweep(packed, left, parts, weights, blocks)
        if rest:
            left = rest[0]
        parts = spread(merge(spread(part, "sample"), groups), "state")
    return finish(group, parts, weights).reshape(-1)


def solution(mesh):
    in_specs = (P(None, "sample"), P(None, "state"), P("sample"), P("state"))
    out_specs = P("state")
    return jax.shard_map(
        per_device, mesh=mesh, in_specs=in_specs, out_specs=out_specs, check_vma=False
    )
```

time: 132 us -> 196 us (1.48)
  Pallas kernels: 37.8 us -> 104 us
    pallas_call x2, Pallas kernels: 28.8 us -> 95 us  [sweep(): pl.pallas_call(functools.partial(sweep_kernel, first), out_shape=[jax.Sha...]
where the time goes in v2:
time: 196 us; the launch traced here: 195 us
  Pallas kernels  104 us (53%)
  blocking collectives  89.3 us (46%)
    pallas_call x2, Pallas kernels, sweep(): pl.pallas_call(functools.partial(sweep_kernel, first), out_shape=[jax.Sha...  95 us
    all_to_all x6, blocking collectives, spread(): return lax.all_to_all(copies, axis, 0, 0)  89.3 us

profile of v2, /device:TPU:1, one launch (start us, length us, event | category | flops | bytes accessed | tf_op | source)
XLA Modules:
  0.0 195.2 jit_solution(13801879007514413077)
XLA Ops:
  0.0 2.5 %prepare.1 = (f32[16,1,256]{2,1,0:T(1,128)}, bf16[2048,128]{1,0:T(8,128)(2,1)}) custom-call(s32[1]{0:T(128)} %bitcast.group_ref, s32[1,32768]{1,0:T(1,128)} %bitcast.4, s32[1,32768]{1,0:T(1,128)} %bitcast.5, bf16[32,32768]{1,0:T(8,128)(2,1)} %energy_ref.1), custom_call_target="tpu_custom_call" | custom-call | tf_op jit(solution)/shard_map/prepare/pallas_call | solution.py:79
  2.5 17.4 %all_to_all.30.counts_ref = f32[16,1,256]{2,1,0:T(1,128)} all-to-all(f32[16,1,256]{2,1,0:T(1,128)} %get-tuple-element.12), channel_id=1, replica_groups=mesh['state'=16,'sample'=16] {'sample'}, dimensions={0} | all-to-all | bytes 32768 | tf_op jit(solution)/shard_map/all_to_all | solution.py:361
  19.9 1.5 pack.1
  21.5 14.7 %all_to_all.31.refs_0_ = bf16[16,40,256]{2,1,0:T(8,128)(2,1)S(1)} all-to-all(bf16[16,40,256]{2,1,0:T(8,128)(2,1)} %pack.1), channel_id=1, replica_groups=mesh['state'=16,'sample'=16] {'state'}, dimensions={0} | all-to-all | bytes 655360 | tf_op jit(solution)/shard_map/all_to_all | solution.py:361
  36.2 0.0 copy-start
  36.2 1.0 copy-done
  37.2 85.1 %first_sweep.1 = (f32[16,32,128]{2,1,0:T(8,128)S(1)}, f32[32,128]{1,0:T(8,128)S(1)}, bf16[2048,128]{1,0:T(8,128)(2,1)S(1)}) custom-call(bf16[16,40,256]{2,1,0:T(8,128)(2,1)S(1)} %all_to_all.31.refs_0_, bf16[2048,128]{1,0:T(8,128)(2,1)S(1)} %copy-done), custom_call_target="tpu_custom_call" | custom-call | tf_op jit(solution)/shard_map/first_sweep/pallas_call | solution.py:326
  122.3 17.2 %all_to_all.32.parts_ref = f32[16,32,128]{2,1,0:T(8,128)} all-to-all(f32[16,32,128]{2,1,0:T(8,128)S(1)} %get-tuple-element.15), channel_id=1, replica_groups=mesh['state'=16,'sample'=16] {'sample'}, dimensions={0} | all-to-all | bytes 524288 | tf_op jit(solution)/shard_map/all_to_all | solution.py:361
  139.5 1.7 merge.2
  141.2 12.1 %all_to_all.33.refs_2_ = f32[16,32,128]{2,1,0:T(8,128)S(1)} all-to-all(f32[16,32,128]{2,1,0:T(8,128)} %merge.2), channel_id=1, replica_groups=mesh['state'=16,'sample'=16] {'state'}, dimensions={0} | all-to-all | bytes 524288 | tf_op jit(solution)/shard_map/all_to_all | solution.py:361
  153.4 9.9 %next_sweep.1 = (f32[16,32,128]{2,1,0:T(8,128)S(1)}, f32[32,128]{1,0:T(8,128)S(1)}) custom-call(bf16[16,40,256]{2,1,0:T(8,128)(2,1)S(1)} %all_to_all.31.refs_0_, bf16[2048,128]{1,0:T(8,128)(2,1)S(1)} %get-tuple-element.14.refs_1_, f32[16,32,128]{2,1,0:T(8,128)S(1)} %all_to_all.33.refs_2_, f32[32,128]{1,0:T(8,128)S(1)} %get-tuple-element.16.refs_3_), custom_call_target="tpu_custom_call" | custom-call | tf_op jit(solution)/shard_map/next_sweep/pallas_call | solution.py:326
  163.3 0.0 copy-start.1
  163.3 0.6 copy-done.1
  163.9 14.9 %all_to_all.34.parts_ref = f32[16,32,128]{2,1,0:T(8,128)} all-to-all(f32[16,32,128]{2,1,0:T(8,128)S(1)} %get-tuple-element.17), channel_id=1, replica_groups=mesh['state'=16,'sample'=16] {'sample'}, dimensions={0} | all-to-all | bytes 524288 | tf_op jit(solution)/shard_map/all_to_all | solution.py:361
  178.8 1.7 merge.3
  180.5 13.1 %all_to_all.35.parts_ref = f32[16,32,128]{2,1,0:T(8,128)} all-to-all(f32[16,32,128]{2,1,0:T(8,128)} %merge.3), channel_id=1, replica_groups=mesh['state'=16,'sample'=16] {'state'}, dimensions={0} | all-to-all | bytes 524288 | tf_op jit(solution)/shard_map/all_to_all | solution.py:361
  193.6 1.7 finish.1
Async XLA Ops:
  36.2 1.0 copy-start
  163.3 0.6 copy-start.1

commit v3 on v2

--- a/solution.py
+++ b/solution.py
@@ -32,18 +32,36 @@
     return high, middle, low
 
 
-def prepare_kernel(group_ref, anchor_ref, own_ref, energy_ref, out_ref, left_ref):
-    base = group_ref[0] * 16
+def live_rows(group, own, live_slots):
+    lane = lax.broadcasted_iota(jnp.int32, (1, LANES), 1)
+    tile = group + 16 * lax.shift_right_logical(lane, 3)
+    slot = tile * LANES + 8 * own + lax.bitwise_and(lane, 7)
+    return slot.astype(jnp.float32) < live_slots
+
+
+def prepare_kernel(place_ref, anchor_ref, energy_ref, out_ref, tile_ref, sems):
+    group = place_ref[0]
+    tiles = tile_ref.shape[0]
+
+    def fetch(i):
+        at = pl.multiple_of((group + tiles * i) * LANES, LANES)
+        return pltpu.make_async_copy(energy_ref.at[:, pl.ds(at, LANES)], tile_ref.at[i], sems.at[i])
+
+    for i in range(tiles):
+        fetch(i).start()
+    base = group * 16
     total = anchor_ref.shape[1]
     step = 4096
     row = lax.broadcasted_iota(jnp.int32, (16, step), 0)
     counts = jnp.zeros((16, 16), jnp.float32)
+    live = jnp.zeros((1, step), jnp.float32)
     for start in range(0, total, step):
         anchor = anchor_ref[:, start : start + step]
         high = lax.shift_right_logical(anchor, 4) - base
         low = lax.bitwise_and(anchor, 15)
         high_hot = jnp.where(row == high, 1.0, 0.0).astype(jnp.bfloat16)
         low_hot = jnp.where(row == low, 1.0, 0.0).astype(jnp.bfloat16)
+        live += jnp.where(anchor < tiles * STATE_TILE, 1.0, 0.0)
         counts += lax.dot_general(
             high_hot, low_hot, (((1,), (1,)), ((), ())), preferred_element_type=jnp.float32
         )
@@ -58,63 +76,93 @@
         precision=lax.Precision.HIGHEST,
     )
     flat = jnp.sum(jnp.where(lax.shift_right_logical(lane, 4) == row16, placed, 0.0), axis=0, keepdims=True)
-    out_ref[...] = jnp.broadcast_to(flat[None], out_ref.shape)
-
-    components, samples = energy_ref.shape
-    live = jnp.where(own_ref[...] < 16 * 256, 1.0, 0.0)
-    energy = energy_ref[...].astype(jnp.float32) * live
-    row = lax.broadcasted_iota(jnp.int32, (DEPTH - 3 * components, samples), 0)
-    ones = row < SHIFT_AT - WEIGHT_AT
-    tail = jnp.where(ones, 1.0, jnp.where(row == LIVE_AT - WEIGHT_AT, live, 0.0))
-    block = jnp.concatenate([energy, energy, energy, tail], axis=0)
-    for at in range(0, samples, 256):
-        left_ref[at : at + 256, :] = block[:, at : at + 256].T.astype(jnp.bfloat16)
-
-
-def prepare(group, anchor, energy, copies, groups):
+    amount = jnp.broadcast_to(jnp.sum(live, axis=1, keepdims=True), (1, LANES))
+
+    def halves(value):
+        high = jnp.floor(value * (1.0 / 256.0))
+        return high, value - high * 256.0
+
+    flat_high, flat_low = halves(flat)
+    rows = [flat_high[:, :LANES], flat_high[:, LANES:], flat_low[:, :LANES], flat_low[:, LANES:]]
+    rows += list(halves(amount)) + [jnp.zeros((2, LANES), jnp.float32)]
+    for i in range(tiles):
+        fetch(i).wait()
+    lane = lax.shift_right_logical(lax.broadcasted_iota(jnp.int32, tile_ref.shape[1:], 1), 3)
+    energies = [tile_ref[i].astype(jnp.float32) for i in range(tiles)]
+    for j in range(out_ref.shape[0]):
+        piece = energies[j]
+        for i in range(tiles):
+            if i != j:
+                piece = jnp.where(lane == i, pltpu.roll(energies[i], (8 * (i - j)) % LANES, 1), piece)
+        out_ref[j] = jnp.concatenate([piece] + rows, axis=0).astype(jnp.bfloat16)
+
+
+def prepare(place, anchor, energy, copies, groups):
     total = anchor.shape[0]
     components = energy.shape[0]
-    share = total // groups
-    row = anchor.reshape(1, total)
     return pl.pallas_call(
         prepare_kernel,
-        out_shape=[
-            jax.ShapeDtypeStruct((copies, 1, 256), jnp.float32),
-            jax.ShapeDtypeStruct((share, DEPTH), jnp.bfloat16),
-        ],
+        out_shape=jax.ShapeDtypeStruct((copies, components + 8, LANES), jnp.bfloat16),
         grid_spec=pltpu.PrefetchScalarGridSpec(
             num_scalar_prefetch=1,
             grid=(1,),
             in_specs=[
                 pl.BlockSpec((1, total), lambda i, g: (0, 0)),
-                pl.BlockSpec((1, share), lambda i, g: (0, g[0])),
-                pl.BlockSpec((components, share), lambda i, g: (0, g[0])),
+                pl.BlockSpec(memory_space=pl.ANY),
             ],
-            out_specs=[
-                pl.BlockSpec((copies, 1, 256), lambda i, g: (0, 0, 0)),
-                pl.BlockSpec((share, DEPTH), lambda i, g: (0, 0)),
+            out_specs=pl.BlockSpec((copies, components + 8, LANES), lambda i, g: (0, 0, 0)),
+            scratch_shapes=[
+                pltpu.VMEM((groups, components, LANES), jnp.bfloat16),
+                pltpu.SemaphoreType.DMA((groups,)),
             ],
         ),
         name="prepare",
-    )(group, row, row, energy)
-
-
-def pack_kernel(counts_ref, start_ref, coef_ref, out_ref):
-    counts = jnp.sum(counts_ref[...], axis=0)
-    log_counts = jnp.log(counts)
-    rows = list(split3(log_counts)) + list(split3(start_ref[...]))
-    rows.append(jnp.zeros((2,) + counts.shape[1:], jnp.float32))
+    )(place, anchor.reshape(1, total), energy)
+
+
+def collect_kernel(place_ref, pieces_ref, start_ref, coef_ref, out_ref, left_ref, amount_ref, wide_ref):
+    components = coef_ref.shape[0]
+    wide_ref[...] = jnp.zeros_like(wide_ref)
+    counts = jnp.zeros((1, STATE_TILE), jnp.float32)
+    lane = lax.broadcasted_iota(jnp.int32, (1, LANES), 1)
+    row = lax.broadcasted_iota(jnp.int32, (DEPTH - 3 * components, LANES), 0)
+    at = jnp.int32(0)
+    for b in range(pieces_ref.shape[0]):
+        piece = pieces_ref[b].astype(jnp.float32)
+        rest = piece[components:]
+        counts += jnp.concatenate([rest[0:1], rest[1:2]], axis=1) * 256.0
+        counts += jnp.concatenate([rest[2:3], rest[3:4]], axis=1)
+        is_live = live_rows(place_ref[0], place_ref[1], rest[4:5] * 256.0 + rest[5:6])
+        live = jnp.where(is_live, 1.0, 0.0)
+        starts = jnp.where(lax.bitwise_and(lane, 7) == 0, live, 0.0)
+        energy = piece[:components] * live
+        tail = jnp.where(row < SHIFT_AT - WEIGHT_AT, 1.0, jnp.where(row == LIVE_AT - WEIGHT_AT, live, 0.0))
+        block = jnp.concatenate([energy, energy, energy, tail], axis=0)
+        wide_ref[pl.ds(pl.multiple_of(at, 8), LANES), :] = block.T
+        at = at + 8 * jnp.sum(starts).astype(jnp.int32)
+    left_ref[...] = wide_ref[...].astype(jnp.bfloat16)
+    amount_ref[0] = at
+    rows = list(split3(jnp.log(counts))) + list(split3(start_ref[...]))
+    rows.append(jnp.zeros((2, STATE_TILE), jnp.float32))
     packed = jnp.concatenate([coef_ref[...].astype(jnp.float32)] + rows, axis=0).astype(jnp.bfloat16)
     out_ref[...] = jnp.broadcast_to(packed[None], out_ref.shape)
 
 
-def pack(counts, f_start, coef, copies):
+def collect(place, pieces, f_start, coef, copies):
     components, states = coef.shape
+    most = pieces.shape[0] * LANES
     return pl.pallas_call(
-        pack_kernel,
-        out_shape=jax.ShapeDtypeStruct((copies, components + 8, states), jnp.bfloat16),
-        name="pack",
-    )(counts, f_start.reshape(1, states), coef)
+        collect_kernel,
+        out_shape=[
+            jax.ShapeDtypeStruct((copies, components + 8, states), jnp.bfloat16),
+            jax.ShapeDtypeStruct((most, DEPTH), jnp.bfloat16),
+            jax.ShapeDtypeStruct((1,), jnp.int32),
+        ],
+        in_specs=[pl.BlockSpec(memory_space=pltpu.SMEM)] + [pl.BlockSpec(memory_space=pltpu.VMEM)] * 3,
+        out_specs=[pl.BlockSpec(memory_space=pltpu.VMEM)] * 2 + [pl.BlockSpec(memory_space=pltpu.SMEM)],
+        scratch_shapes=[pltpu.VMEM((most, DEPTH), jnp.float32)],
+        name="collect",
+    )(place, pieces, f_start.reshape(1, states), coef)
 
 
 def merge_logs(parts):
@@ -149,17 +197,17 @@
 
 def sweep_kernel(first, *refs):
     if first:
-        packed_ref, left_ref, part_ref, wide_ref, shifted_ref, right_ref, scaled_ref, acc_ref, some_ref, norm_ref, top_ref = refs
+        amount_ref, packed_ref, left_ref, part_ref, wide_ref, shifted_ref, right_ref, scaled_ref, acc_ref, some_ref, norm_ref, top_ref = refs
         source_ref = shifted_ref
     else:
-        packed_ref, left_ref, parts_ref, old_ref, part_ref, wide_ref, some_ref, right_ref, scaled_ref, acc_ref, norm_ref, top_ref = refs
+        amount_ref, packed_ref, left_ref, parts_ref, old_ref, part_ref, wide_ref, some_ref, right_ref, scaled_ref, acc_ref, norm_ref, top_ref = refs
         source_ref = left_ref
     groups, packed_rows, _ = packed_ref.shape
     components = packed_rows - 8
-    samples = left_ref.shape[0]
     states = groups * STATE_TILE
     pair = STATE_TILE // LANES
-    tiles = samples // ROW_TILE
+    amount = amount_ref[0]
+    tiles = (amount + ROW_TILE - 1) // ROW_TILE
 
     for g in range(groups):
         rows = packed_ref[g, components:, :].astype(jnp.float32)
@@ -244,7 +292,7 @@
     most = jnp.max(most)
     sums = jnp.sum(acc_ref[...], axis=0, keepdims=True)
     smallest = jnp.min(sums)
-    some_live = jnp.max(left_ref[:, LIVE_AT : LIVE_AT + 1].astype(jnp.float32)) > 0.0
+    some_live = amount > 0
     logs = jnp.where(sums > 0.0, jnp.log2(jnp.maximum(sums, SAFE_SUM)), LOW)
 
     def give(value):
@@ -299,17 +347,12 @@
         give(top_ref[...] + jnp.log2(acc_ref[0:1, :]))
 
 
-def whole(shape):
-    return pl.BlockSpec(shape, lambda: (0,) * len(shape))
-
-
-def sweep(packed, left, parts, old, copies):
+def sweep(amount, packed, left, parts, old, copies):
     groups = packed.shape[0]
     states = groups * STATE_TILE
-    samples = left.shape[0]
     first = parts is None
     tall = states // LANES
-    operands = [packed, left] + ([] if first else [parts, old])
+    operands = [amount, packed, left] + ([] if first else [parts, old])
     outs = [((copies, tall, LANES), jnp.float32), ((tall, LANES), jnp.float32)]
     scratch = [
         pltpu.VMEM((DEPTH, states), jnp.bfloat16),
@@ -326,6 +369,7 @@
     return pl.pallas_call(
         functools.partial(sweep_kernel, first),
         out_shape=[jax.ShapeDtypeStruct(*out) for out in outs],
+        in_specs=[pl.BlockSpec(memory_space=pltpu.SMEM)] + [pl.BlockSpec(memory_space=pltpu.VMEM)] * (len(operands) - 1),
         scratch_shapes=scratch,
         compiler_params=pltpu.CompilerParams(vmem_limit_bytes=40 * 2**20),
         name="first_sweep" if first else "next_sweep",
@@ -364,18 +408,18 @@
 def per_device(energy, coef, anchor, f_start):
     groups = lax.axis_size("state")
     blocks = lax.axis_size("sample")
-    group = lax.axis_index("state").astype(jnp.int32).reshape(1)
-    counts, left = prepare(group, anchor, energy, blocks, groups)
-    counts = spread(counts, "sample")
-    packed = spread(pack(counts, f_start, coef, groups), "state")
+    place = jnp.stack([lax.axis_index("state"), lax.axis_index("sample")]).astype(jnp.int32)
+    pieces = spread(prepare(place, anchor, energy, blocks, groups), "sample")
+    packed, left, amount = collect(place, pieces, f_start, coef, groups)
+    packed = spread(packed, "state")
     parts = None
     weights = None
     for iteration in range(ITERS):
-        part, weights, *rest = sweep(packed, left, parts, weights, blocks)
+        part, weights, *rest = sweep(amount, packed, left, parts, weights, blocks)
         if rest:
             left = rest[0]
         parts = spread(merge(spread(part, "sample"), groups), "state")
-    return finish(group, parts, weights).reshape(-1)
+    return finish(place, parts, weights).reshape(-1)
 
 
 def solution(mesh):

time: 196 us -> 157 us (0.80)
  Pallas kernels: 104 us -> 61.6 us
  blocking collectives: 89.3 us -> 92.5 us
    pallas_call x2, Pallas kernels: 95 us -> 49.8 us  [sweep(): pl.pallas_call(functools.partial(sweep_kernel, first), out_shape=[jax.Sha...]
    all_to_all x6, blocking collectives: 89.3 us -> 92.5 us  [spread(): return lax.all_to_all(copies, axis, 0, 0)]
    pallas_call x2, Pallas kernels: 4.04 us -> 6.06 us  [the longest x1 3.82 us: prepare(): pl.pallas_call(prepare_kernel, out_shape=jax.ShapeDtypeStruct((copies, co...]
where the time goes in v3:
time: 157 us; the launch traced here: 156 us
  blocking collectives  92.5 us (59%)
  Pallas kernels  61.6 us (39%)
  local copies, waits for them, and re-layouts  1.63 us (1%)
    all_to_all x6, blocking collectives, spread(): return lax.all_to_all(copies, axis, 0, 0)  92.5 us
    pallas_call x2, Pallas kernels, sweep(): pl.pallas_call(functools.partial(sweep_kernel, first), out_shape=[jax.Sha...  49.8 us
    pallas_call x1, Pallas kernels, prepare(): pl.pallas_call(prepare_kernel, out_shape=jax.ShapeDtypeStruct((copies, co...  3.82 us
    pallas_call x2, Pallas kernels, merge(): pl.pallas_call(merge_kernel, out_shape=jax.ShapeDtypeStruct((copies,) + p...  3.46 us

profile of v3, /device:TPU:1, one launch (start us, length us, event | category | flops | bytes accessed | tf_op | source)
XLA Modules:
  0.0 156.4 jit_solution(17098285976322590209)
XLA Ops:
  0.0 0.6 pad_add_fusion.place_ref.group_ref
  0.6 3.8 %prepare.1 = bf16[16,40,128]{2,1,0:T(8,128)(2,1)} custom-call(s32[2]{0:T(128)} %pad_add_fusion.place_ref.group_ref, s32[1,32768]{1,0:T(1,128)} %bitcast.5, bf16[32,32768]{1,0:T(8,128)(2,1)} %energy_ref.1), custom_call_target="tpu_custom_call" | custom-call | tf_op jit(solution)/shard_map/prepare/pallas_call | solution.py:103
  4.5 19.7 %all_to_all.30.pieces_ref = bf16[16,40,128]{2,1,0:T(8,128)(2,1)} all-to-all(bf16[16,40,128]{2,1,0:T(8,128)(2,1)} %prepare.1), channel_id=1, replica_groups=mesh['state'=16,'sample'=16] {'sample'}, dimensions={0} | all-to-all | bytes 327680 | tf_op jit(solution)/shard_map/all_to_all | solution.py:405
  24.2 2.2 %collect.1 = (bf16[16,40,256]{2,1,0:T(8,128)(2,1)}, bf16[2048,128]{1,0:T(8,128)(2,1)}, s32[1]{0:T(128)}) custom-call(s32[2]{0:T(128)} %pad_add_fusion.place_ref.group_ref, bf16[16,40,128]{2,1,0:T(8,128)(2,1)} %all_to_all.30.pieces_ref, f32[1,256]{1,0:T(1,128)} %bitcast.6, bf16[32,256]{1,0:T(8,128)(2,1)} %coef_ref.1), custom_call_target="tpu_custom_call" | custom-call | tf_op jit(solution)/shard_map/collect/pallas_call | solution.py:154
  26.5 15.4 %all_to_all.31.refs_1_ = bf16[16,40,256]{2,1,0:T(8,128)(2,1)S(1)} all-to-all(bf16[16,40,256]{2,1,0:T(8,128)(2,1)} %get-tuple-element.14), channel_id=1, replica_groups=mesh['state'=16,'sample'=16] {'state'}, dimensions={0} | all-to-all | bytes 655360 | tf_op jit(solution)/shard_map/all_to_all | solution.py:405
  41.8 0.0 copy-start
  41.8 1.0 copy-done
  42.9 43.8 %first_sweep.1 = (f32[16,32,128]{2,1,0:T(8,128)S(1)}, f32[32,128]{1,0:T(8,128)S(1)}, bf16[2048,128]{1,0:T(8,128)(2,1)S(1)}) custom-call(s32[1]{0:T(128)} %get-tuple-element.13.refs_0_, bf16[16,40,256]{2,1,0:T(8,128)(2,1)S(1)} %all_to_all.31.refs_1_, bf16[2048,128]{1,0:T(8,128)(2,1)S(1)} %copy-done), custom_call_target="tpu_custom_call" | custom-call | tf_op jit(solution)/shard_map/first_sweep/pallas_call | solution.py:369
  86.6 16.5 %all_to_all.32.parts_ref = f32[16,32,128]{2,1,0:T(8,128)} all-to-all(f32[16,32,128]{2,1,0:T(8,128)S(1)} %get-tuple-element.17), channel_id=1, replica_groups=mesh['state'=16,'sample'=16] {'sample'}, dimensions={0} | all-to-all | bytes 524288 | tf_op jit(solution)/shard_map/all_to_all | solution.py:405
  103.1 1.7 %merge.2 = f32[16,32,128]{2,1,0:T(8,128)} custom-call(f32[16,32,128]{2,1,0:T(8,128)} %all_to_all.32.parts_ref), custom_call_target="tpu_custom_call" | custom-call | tf_op jit(solution)/shard_map/merge/pallas_call | solution.py:178
  104.8 12.7 %all_to_all.33.refs_3_ = f32[16,32,128]{2,1,0:T(8,128)S(1)} all-to-all(f32[16,32,128]{2,1,0:T(8,128)} %merge.2), channel_id=1, replica_groups=mesh['state'=16,'sample'=16] {'state'}, dimensions={0} | all-to-all | bytes 524288 | tf_op jit(solution)/shard_map/all_to_all | solution.py:405
  117.6 6.0 %next_sweep.1 = (f32[16,32,128]{2,1,0:T(8,128)S(1)}, f32[32,128]{1,0:T(8,128)S(1)}) custom-call(s32[1]{0:T(128)} %get-tuple-element.13.refs_0_, bf16[16,40,256]{2,1,0:T(8,128)(2,1)S(1)} %all_to_all.31.refs_1_, bf16[2048,128]{1,0:T(8,128)(2,1)S(1)} %get-tuple-element.16.refs_2_, f32[16,32,128]{2,1,0:T(8,128)S(1)} %all_to_all.33.refs_3_, ...), custom_call_target="tpu_custom_call" | custom-call | tf_op jit(solution)/shard_map/next_sweep/pallas_call | solution.py:369
  123.6 0.0 copy-start.1
  123.6 0.6 copy-done.1
  124.2 15.3 %all_to_all.34.parts_ref = f32[16,32,128]{2,1,0:T(8,128)} all-to-all(f32[16,32,128]{2,1,0:T(8,128)S(1)} %get-tuple-element.19), channel_id=1, replica_groups=mesh['state'=16,'sample'=16] {'sample'}, dimensions={0} | all-to-all | bytes 524288 | tf_op jit(solution)/shard_map/all_to_all | solution.py:405
  139.5 1.7 %merge.3 = f32[16,32,128]{2,1,0:T(8,128)} custom-call(f32[16,32,128]{2,1,0:T(8,128)} %all_to_all.34.parts_ref), custom_call_target="tpu_custom_call" | custom-call | tf_op jit(solution)/shard_map/merge/pallas_call | solution.py:178
  141.2 12.8 %all_to_all.35.parts_ref = f32[16,32,128]{2,1,0:T(8,128)} all-to-all(f32[16,32,128]{2,1,0:T(8,128)} %merge.3), channel_id=1, replica_groups=mesh['state'=16,'sample'=16] {'state'}, dimensions={0} | all-to-all | bytes 524288 | tf_op jit(solution)/shard_map/all_to_all | solution.py:405
  154.1 2.3 %finish.1 = f32[2,128]{1,0:T(2,128)} custom-call(s32[2]{0:T(128)} %pad_add_fusion.place_ref.group_ref, f32[16,32,128]{2,1,0:T(8,128)} %all_to_all.35.parts_ref, f32[32,128]{1,0:T(8,128)} %copy-done.1), custom_call_target="tpu_custom_call" | custom-call | tf_op jit(solution)/shard_map/finish/pallas_call | solution.py:387
Async XLA Ops:
  41.8 1.0 copy-start
  123.6 0.6 copy-start.1

commit v4 on v3

--- a/solution.py
+++ b/solution.py
@@ -17,7 +17,7 @@
 
 LANES = 128
 STATE_TILE = 256
-ROW_TILE = 512
+ROW_TILE = 416
 DEPTH = 128
 WEIGHT_AT = 96
 SHIFT_AT = 99
@@ -39,8 +39,8 @@
     return slot.astype(jnp.float32) < live_slots
 
 
-def prepare_kernel(place_ref, anchor_ref, energy_ref, out_ref, tile_ref, sems):
-    group = place_ref[0]
+def prepare_kernel(group_ref, anchor_ref, energy_ref, out_ref, tile_ref, sems):
+    group = group_ref[0]
     tiles = tile_ref.shape[0]
 
     def fetch(i):
@@ -97,7 +97,7 @@
         out_ref[j] = jnp.concatenate([piece] + rows, axis=0).astype(jnp.bfloat16)
 
 
-def prepare(place, anchor, energy, copies, groups):
+def prepare(group, anchor, energy, copies, groups):
     total = anchor.shape[0]
     components = energy.shape[0]
     return pl.pallas_call(
@@ -108,7 +108,7 @@
             grid=(1,),
             in_specs=[
                 pl.BlockSpec((1, total), lambda i, g: (0, 0)),
-                pl.BlockSpec(memory_space=pl.ANY),
+                pl.BlockSpec(memory_space=pltpu.HBM),
             ],
             out_specs=pl.BlockSpec((copies, components + 8, LANES), lambda i, g: (0, 0, 0)),
             scratch_shapes=[
@@ -116,23 +116,21 @@
                 pltpu.SemaphoreType.DMA((groups,)),
             ],
         ),
+        compiler_params=pltpu.CompilerParams(vmem_limit_bytes=56 * 2**20),
         name="prepare",
-    )(place, anchor.reshape(1, total), energy)
-
-
-def collect_kernel(place_ref, pieces_ref, start_ref, coef_ref, out_ref, left_ref, amount_ref, wide_ref):
-    components = coef_ref.shape[0]
+    )(group, anchor.reshape(1, total), energy)
+
+
+def arrange_kernel(group_ref, own_ref, pieces_ref, left_ref, amount_ref, wide_ref):
+    components = pieces_ref.shape[1] - 8
     wide_ref[...] = jnp.zeros_like(wide_ref)
-    counts = jnp.zeros((1, STATE_TILE), jnp.float32)
     lane = lax.broadcasted_iota(jnp.int32, (1, LANES), 1)
     row = lax.broadcasted_iota(jnp.int32, (DEPTH - 3 * components, LANES), 0)
     at = jnp.int32(0)
     for b in range(pieces_ref.shape[0]):
         piece = pieces_ref[b].astype(jnp.float32)
         rest = piece[components:]
-        counts += jnp.concatenate([rest[0:1], rest[1:2]], axis=1) * 256.0
-        counts += jnp.concatenate([rest[2:3], rest[3:4]], axis=1)
-        is_live = live_rows(place_ref[0], place_ref[1], rest[4:5] * 256.0 + rest[5:6])
+        is_live = live_rows(group_ref[0], own_ref[0], rest[4:5] * 256.0 + rest[5:6])
         live = jnp.where(is_live, 1.0, 0.0)
         starts = jnp.where(lax.bitwise_and(lane, 7) == 0, live, 0.0)
         energy = piece[:components] * live
@@ -142,27 +140,46 @@
         at = at + 8 * jnp.sum(starts).astype(jnp.int32)
     left_ref[...] = wide_ref[...].astype(jnp.bfloat16)
     amount_ref[0] = at
+
+
+def arrange(group, own, pieces):
+    most = pl.cdiv(pieces.shape[0] * LANES, ROW_TILE) * ROW_TILE
+    smem = pl.BlockSpec(memory_space=pltpu.SMEM)
+    vmem = pl.BlockSpec(memory_space=pltpu.VMEM)
+    return pl.pallas_call(
+        arrange_kernel,
+        out_shape=[
+            jax.ShapeDtypeStruct((most, DEPTH), jnp.bfloat16),
+            jax.ShapeDtypeStruct((1,), jnp.int32),
+        ],
+        in_specs=[smem, smem, vmem],
+        out_specs=[vmem, smem],
+        scratch_shapes=[pltpu.VMEM((most, DEPTH), jnp.float32)],
+        compiler_params=pltpu.CompilerParams(vmem_limit_bytes=6 * 2**20),
+        name="arrange",
+    )(group, own, pieces)
+
+
+def pack_kernel(pieces_ref, start_ref, coef_ref, out_ref):
+    components = coef_ref.shape[0]
+    counts = jnp.sum(pieces_ref[:, components:, :].astype(jnp.float32), axis=0)
+    counts = jnp.concatenate([counts[0:1], counts[1:2]], axis=1) * 256.0 + jnp.concatenate(
+        [counts[2:3], counts[3:4]], axis=1
+    )
     rows = list(split3(jnp.log(counts))) + list(split3(start_ref[...]))
     rows.append(jnp.zeros((2, STATE_TILE), jnp.float32))
     packed = jnp.concatenate([coef_ref[...].astype(jnp.float32)] + rows, axis=0).astype(jnp.bfloat16)
     out_ref[...] = jnp.broadcast_to(packed[None], out_ref.shape)
 
 
-def collect(place, pieces, f_start, coef, copies):
+def pack(pieces, f_start, coef, copies):
     components, states = coef.shape
-    most = pieces.shape[0] * LANES
-    return pl.pallas_call(
-        collect_kernel,
-        out_shape=[
-            jax.ShapeDtypeStruct((copies, components + 8, states), jnp.bfloat16),
-            jax.ShapeDtypeStruct((most, DEPTH), jnp.bfloat16),
-            jax.ShapeDtypeStruct((1,), jnp.int32),
-        ],
-        in_specs=[pl.BlockSpec(memory_space=pltpu.SMEM)] + [pl.BlockSpec(memory_space=pltpu.VMEM)] * 3,
-        out_specs=[pl.BlockSpec(memory_space=pltpu.VMEM)] * 2 + [pl.BlockSpec(memory_space=pltpu.SMEM)],
-        scratch_shapes=[pltpu.VMEM((most, DEPTH), jnp.float32)],
-        name="collect",
-    )(place, pieces, f_start.reshape(1, states), coef)
+    return pl.pallas_call(
+        pack_kernel,
+        out_shape=jax.ShapeDtypeStruct((copies, components + 8, states), jnp.bfloat16),
+        compiler_params=pltpu.CompilerParams(vmem_limit_bytes=4 * 2**20),
+        name="pack",
+    )(pieces, f_start.reshape(1, states), coef)
 
 
 def merge_logs(parts):
@@ -178,6 +195,7 @@
     return pl.pallas_call(
         merge_kernel,
         out_shape=jax.ShapeDtypeStruct((copies,) + parts.shape[1:], jnp.float32),
+        compiler_params=pltpu.CompilerParams(vmem_limit_bytes=4 * 2**20),
         name="merge",
     )(parts)
 
@@ -197,10 +215,10 @@
 
 def sweep_kernel(first, *refs):
     if first:
-        amount_ref, packed_ref, left_ref, part_ref, wide_ref, shifted_ref, right_ref, scaled_ref, acc_ref, some_ref, norm_ref, top_ref = refs
+        amount_ref, packed_ref, left_ref, part_ref, wide_ref, shifted_ref, right_ref, scaled_ref, acc_ref, some_ref, tall_ref, top_ref = refs
         source_ref = shifted_ref
     else:
-        amount_ref, packed_ref, left_ref, parts_ref, old_ref, part_ref, wide_ref, some_ref, right_ref, scaled_ref, acc_ref, norm_ref, top_ref = refs
+        amount_ref, packed_ref, left_ref, parts_ref, old_ref, part_ref, wide_ref, some_ref, right_ref, scaled_ref, acc_ref, tall_ref, top_ref = refs
         source_ref = left_ref
     groups, packed_rows, _ = packed_ref.shape
     components = packed_rows - 8
@@ -288,23 +306,23 @@
 
     unit = jnp.ones((ROW_TILE, 1), jnp.float32)
     least, most = lax.fori_loop(0, tiles, visit, (unit, unit))
-    least = jnp.min(least)
-    most = jnp.max(most)
+    least = jnp.min(least, axis=0, keepdims=True)
+    most = jnp.max(most, axis=0, keepdims=True)
     sums = jnp.sum(acc_ref[...], axis=0, keepdims=True)
-    smallest = jnp.min(sums)
-    some_live = amount > 0
+    smallest = jnp.min(sums, axis=1, keepdims=True)
     logs = jnp.where(sums > 0.0, jnp.log2(jnp.maximum(sums, SAFE_SUM)), LOW)
 
     def give(value):
         for k in range(states // LANES):
-            piece = value[:, k * LANES : (k + 1) * LANES]
-            part_ref[:, k : k + 1, :] = jnp.broadcast_to(piece[None], (part_ref.shape[0], 1, LANES))
+            tall_ref[k : k + 1, :] = value[:, k * LANES : (k + 1) * LANES]
+        part_ref[...] = jnp.broadcast_to(tall_ref[...][None], part_ref.shape)
 
     give(logs)
     enough = jnp.logical_and(smallest >= SAFE_SUM, smallest * least >= SAFE_SUM)
     safe = jnp.logical_and(enough, jnp.logical_and(most < SAFE_TOP, least > SAFE_SUM))
-
-    @pl.when(jnp.logical_and(some_live, jnp.logical_not(safe)))
+    unsafe = jnp.max(jnp.where(safe, 0.0, 1.0)) > 0.0
+
+    @pl.when(jnp.logical_and(amount > 0, unsafe))
     def exact():
         acc_ref[...] = jnp.zeros_like(acc_ref)
         top_ref[...] = jnp.full_like(top_ref, LOW)
@@ -359,7 +377,7 @@
         pltpu.VMEM((ROW_TILE, states), jnp.float32),
         pltpu.VMEM((8, states), jnp.float32),
         pltpu.VMEM((DEPTH, 2 * LANES), jnp.bfloat16),
-        pltpu.VMEM((8, LANES), jnp.float32),
+        pltpu.VMEM((tall, LANES), jnp.float32),
         pltpu.VMEM((1, states), jnp.float32),
     ]
     if first:
@@ -371,7 +389,7 @@
         out_shape=[jax.ShapeDtypeStruct(*out) for out in outs],
         in_specs=[pl.BlockSpec(memory_space=pltpu.SMEM)] + [pl.BlockSpec(memory_space=pltpu.VMEM)] * (len(operands) - 1),
         scratch_shapes=scratch,
-        compiler_params=pltpu.CompilerParams(vmem_limit_bytes=40 * 2**20),
+        compiler_params=pltpu.CompilerParams(vmem_limit_bytes=20 * 2**20),
         name="first_sweep" if first else "next_sweep",
     )(*operands)
 
@@ -397,6 +415,7 @@
             out_specs=pl.BlockSpec((rows, LANES), lambda i, g: (0, 0)),
             scratch_shapes=[pltpu.VMEM(old.shape, jnp.float32)],
         ),
+        compiler_params=pltpu.CompilerParams(vmem_limit_bytes=4 * 2**20),
         name="finish",
     )(group, parts, old)
 
@@ -408,10 +427,11 @@
 def per_device(energy, coef, anchor, f_start):
     groups = lax.axis_size("state")
     blocks = lax.axis_size("sample")
-    place = jnp.stack([lax.axis_index("state"), lax.axis_index("sample")]).astype(jnp.int32)
-    pieces = spread(prepare(place, anchor, energy, blocks, groups), "sample")
-    packed, left, amount = collect(place, pieces, f_start, coef, groups)
-    packed = spread(packed, "state")
+    group = lax.axis_index("state").astype(jnp.int32).reshape(1)
+    own = lax.axis_index("sample").astype(jnp.int32).reshape(1)
+    pieces = spread(prepare(group, anchor, energy, blocks, groups), "sample")
+    packed = spread(pack(pieces, f_start, coef, groups), "state")
+    left, amount = arrange(group, own, pieces)
     parts = None
     weights = None
     for iteration in range(ITERS):
@@ -419,7 +439,7 @@
         if rest:
             left = rest[0]
         parts = spread(merge(spread(part, "sample"), groups), "state")
-    return finish(place, parts, weights).reshape(-1)
+    return finish(group, parts, weights).reshape(-1)
 
 
 def solution(mesh):

time: 157 us -> 139 us (0.89)
  blocking collectives: 92.5 us -> 74 us
  Pallas kernels: 61.6 us -> 49.7 us
  waiting for transfers between devices: 0 us -> 7.73 us
  starting transfers between devices: 0 us -> 6.75 us
  local copies, waits for them, and re-layouts: 1.63 us -> 0.01 us
    all_to_all x6 -> x5, blocking collectives: 92.5 us -> 74 us  [spread(): return lax.all_to_all(copies, axis, 0, 0)]
    all_to_all x0 -> x1, waiting for transfers between devices: none -> 7.73 us  [spread(): return lax.all_to_all(copies, axis, 0, 0)]
    all_to_all x0 -> x1, starting transfers between devices: none -> 6.75 us  [spread(): return lax.all_to_all(copies, axis, 0, 0)]
    pallas_call x2, Pallas kernels: 49.8 us -> 44 us  [sweep(): pl.pallas_call(functools.partial(sweep_kernel, first), out_shape=[jax.Sha...]
    pallas_call x2, Pallas kernels: 3.46 us -> 0.14 us  [merge(): pl.pallas_call(merge_kernel, out_shape=jax.ShapeDtypeStruct((copies,) + p...]
    unnamed x4, local copies, waits for them, and re-layouts: 1.63 us -> 0.01 us
    pallas_call x1, Pallas kernels: 2.33 us -> 0.72 us  [finish(): pl.pallas_call(finish_kernel, out_shape=jax.ShapeDtypeStruct((rows, LANES...]
  transfers between devices with their start and end apart: 0 -> 1, of which waited for: 0 -> 1; matrix products, arithmetic and copies ran while one was open for 0% -> 0% of each run, Pallas kernels for 0% -> 1%
where the time goes in v4:
time: 139 us; the launch traced here: 138 us
  blocking collectives  74 us (53%)
  Pallas kernels  49.7 us (36%)
  waiting for transfers between devices  7.73 us (6%)
  starting transfers between devices  6.75 us (5%)
    all_to_all x5, blocking collectives, spread(): return lax.all_to_all(copies, axis, 0, 0)  74 us
    pallas_call x2, Pallas kernels, sweep(): pl.pallas_call(functools.partial(sweep_kernel, first), out_shape=[jax.Sha...  44 us
    all_to_all x1, waiting for transfers between devices, spread(): return lax.all_to_all(copies, axis, 0, 0)  7.73 us
    all_to_all x1, starting transfers between devices, spread(): return lax.all_to_all(copies, axis, 0, 0)  6.75 us
    pallas_call x1, Pallas kernels, prepare(): pl.pallas_call(prepare_kernel, out_shape=jax.ShapeDtypeStruct((copies, co...  3.2 us
  transfers between devices with their start and end apart: 1, of which 1 were waited for; matrix products, arithmetic and copies ran while one was open for 0% of the time, Pallas kernels for 1%

profile of v4, /device:TPU:1, one launch (start us, length us, event | category | flops | bytes accessed | tf_op | source)
XLA Modules:
  0.0 138.2 jit_solution(11704087049230401579)
XLA Ops:
  0.0 0.0 copy-start.1
  0.0 0.0 copy-start
  0.0 3.2 %prepare.1 = bf16[16,40,128]{2,1,0:T(8,128)(2,1)} custom-call(s32[1]{0:T(128)} %bitcast.group_ref, s32[1,32768]{1,0:T(1,128)} %bitcast.6, bf16[32,32768]{1,0:T(8,128)(2,1)} %energy_ref.1), custom_call_target="tpu_custom_call" | custom-call | tf_op jit(solution)/shard_map/prepare/pallas_call | solution.py:103
  3.2 19.6 %all_to_all.30.pieces_ref = bf16[16,40,128]{2,1,0:T(8,128)(2,1)S(1)} all-to-all(bf16[16,40,128]{2,1,0:T(8,128)(2,1)} %prepare.1), channel_id=1, replica_groups=mesh['state'=16,'sample'=16] {'sample'}, dimensions={0} | all-to-all | bytes 327680 | tf_op jit(solution)/shard_map/all_to_all | solution.py:424
  22.8 0.0 copy-done.1
  22.8 0.0 copy-done
  22.9 0.8 pack.1
  23.7 6.8 %all-to-all-start.1 = ((bf16[16,40,256]{2,1,0:T(8,128)(2,1)}), bf16[16,40,256]{2,1,0:T(8,128)(2,1)S(1)}, u32[]{:S(2)}, u32[]{:S(2)}) async-start(bf16[16,40,256]{2,1,0:T(8,128)(2,1)} %pack.1), calls=%async_computation.1 | async-start | bytes 655360 | tf_op jit(solution)/shard_map/all_to_all | solution.py:424
  30.4 0.9 arrange.1
  31.3 7.7 %all-to-all-done.1.refs_1_ = bf16[16,40,256]{2,1,0:T(8,128)(2,1)S(1)} async-done(((bf16[16,40,256]{2,1,0:T(8,128)(2,1)}), bf16[16,40,256]{2,1,0:T(8,128)(2,1)S(1)}, u32[]{:S(2)}, u32[]{:S(2)}) %all-to-all-start.1) | async-done | bytes 327712 | tf_op jit(solution)/shard_map/all_to_all | solution.py:424
  39.0 39.0 %first_sweep.1 = (f32[16,32,128]{2,1,0:T(8,128)S(1)}, f32[32,128]{1,0:T(8,128)S(1)}, bf16[2080,128]{1,0:T(8,128)(2,1)S(1)}) custom-call(s32[1]{0:T(128)} %get-tuple-element.12.refs_0_, bf16[16,40,256]{2,1,0:T(8,128)(2,1)S(1)} %all-to-all-done.1.refs_1_, bf16[2080,128]{1,0:T(8,128)(2,1)S(1)} %get-tuple-element.13.refs_2_), custom_call_target="tpu_custom_call" | custom-call | tf_op jit(solution)/shard_map/first_sweep/pallas_call | solution.py:387
  78.0 15.8 %all_to_all.31.parts_ref = f32[16,32,128]{2,1,0:T(8,128)S(1)} all-to-all(f32[16,32,128]{2,1,0:T(8,128)S(1)} %get-tuple-element.15), channel_id=1, replica_groups=mesh['state'=16,'sample'=16] {'sample'}, dimensions={0} | all-to-all | bytes 524288 | tf_op jit(solution)/shard_map/all_to_all | solution.py:424
  93.8 0.1 merge.2
  93.9 11.7 %all_to_all.32.refs_3_ = f32[16,32,128]{2,1,0:T(8,128)S(1)} all-to-all(f32[16,32,128]{2,1,0:T(8,128)S(1)} %merge.2), channel_id=1, replica_groups=mesh['state'=16,'sample'=16] {'state'}, dimensions={0} | all-to-all | bytes 524288 | tf_op jit(solution)/shard_map/all_to_all | solution.py:424
  105.5 5.0 %next_sweep.1 = (f32[16,32,128]{2,1,0:T(8,128)S(1)}, f32[32,128]{1,0:T(8,128)S(1)}) custom-call(s32[1]{0:T(128)} %get-tuple-element.12.refs_0_, bf16[16,40,256]{2,1,0:T(8,128)(2,1)S(1)} %all-to-all-done.1.refs_1_, bf16[2080,128]{1,0:T(8,128)(2,1)S(1)} %get-tuple-element.14.refs_2_, f32[16,32,128]{2,1,0:T(8,128)S(1)} %all_to_all.32.refs_3_, ...), custom_call_target="tpu_custom_call" | custom-call | tf_op jit(solution)/shard_map/next_sweep/pallas_call | solution.py:387
  110.5 15.4 %all_to_all.33.parts_ref = f32[16,32,128]{2,1,0:T(8,128)S(1)} all-to-all(f32[16,32,128]{2,1,0:T(8,128)S(1)} %get-tuple-element.17), channel_id=1, replica_groups=mesh['state'=16,'sample'=16] {'sample'}, dimensions={0} | all-to-all | bytes 524288 | tf_op jit(solution)/shard_map/all_to_all | solution.py:424
  125.9 0.1 merge.3
  126.0 11.5 %all_to_all.34.parts_ref = f32[16,32,128]{2,1,0:T(8,128)S(1)} all-to-all(f32[16,32,128]{2,1,0:T(8,128)S(1)} %merge.3), channel_id=1, replica_groups=mesh['state'=16,'sample'=16] {'state'}, dimensions={0} | all-to-all | bytes 524288 | tf_op jit(solution)/shard_map/all_to_all | solution.py:424
  137.5 0.7 finish.1
Async XLA Ops:
  0.0 22.8 %copy-start.1 = (f32[256]{0:T(256)S(1)}, f32[256]{0:T(256)}, u32[]{:S(2)}) copy-start(f32[256]{0:T(256)} %param.7) | copy-start | bytes 3076
  0.0 22.8 %copy-start = (bf16[32,256]{1,0:T(8,128)(2,1)S(1)}, bf16[32,256]{1,0:T(8,128)(2,1)}, u32[]{:S(2)}) copy-start(bf16[32,256]{1,0:T(8,128)(2,1)} %coef_ref.1) | copy-start | bytes 49156
  23.7 15.4 %all-to-all-start.1 = ((bf16[16,40,256]{2,1,0:T(8,128)(2,1)}), bf16[16,40,256]{2,1,0:T(8,128)(2,1)S(1)}, u32[]{:S(2)}, u32[]{:S(2)}) async-start(bf16[16,40,256]{2,1,0:T(8,128)(2,1)} %pack.1), calls=%async_computation.1 | async-start | bytes 655360 | tf_op jit(solution)/shard_map/all_to_all | solution.py:424

commit v5 on v4

--- a/solution.py
+++ b/solution.py
@@ -42,6 +42,7 @@
 def prepare_kernel(group_ref, anchor_ref, energy_ref, out_ref, tile_ref, sems):
     group = group_ref[0]
     tiles = tile_ref.shape[0]
+    tall = tiles * STATE_TILE // LANES
 
     def fetch(i):
         at = pl.multiple_of((group + tiles * i) * LANES, LANES)
@@ -49,42 +50,27 @@
 
     for i in range(tiles):
         fetch(i).start()
-    base = group * 16
     total = anchor_ref.shape[1]
-    step = 4096
-    row = lax.broadcasted_iota(jnp.int32, (16, step), 0)
-    counts = jnp.zeros((16, 16), jnp.float32)
-    live = jnp.zeros((1, step), jnp.float32)
+    step = 2048
+    tall_row = lax.broadcasted_iota(jnp.int32, (tall, step), 0)
+    lane_row = lax.broadcasted_iota(jnp.int32, (LANES, step), 0)
+    counts = jnp.zeros((tall, LANES), jnp.float32)
     for start in range(0, total, step):
         anchor = anchor_ref[:, start : start + step]
-        high = lax.shift_right_logical(anchor, 4) - base
-        low = lax.bitwise_and(anchor, 15)
-        high_hot = jnp.where(row == high, 1.0, 0.0).astype(jnp.bfloat16)
-        low_hot = jnp.where(row == low, 1.0, 0.0).astype(jnp.bfloat16)
-        live += jnp.where(anchor < tiles * STATE_TILE, 1.0, 0.0)
+        high = lax.shift_right_logical(anchor, 7)
+        low = lax.bitwise_and(anchor, LANES - 1)
+        high_hot = jnp.where(tall_row == high, 1.0, 0.0).astype(jnp.bfloat16)
+        low_hot = jnp.where(lane_row == low, 1.0, 0.0).astype(jnp.bfloat16)
         counts += lax.dot_general(
             high_hot, low_hot, (((1,), (1,)), ((), ())), preferred_element_type=jnp.float32
         )
-    lane = lax.broadcasted_iota(jnp.int32, (16, 256), 1)
-    row16 = lax.broadcasted_iota(jnp.int32, (16, 256), 0)
-    spread_out = jnp.where(lax.bitwise_and(lane, 15) == row16, 1.0, 0.0)
-    placed = lax.dot_general(
-        counts,
-        spread_out,
-        (((1,), (0,)), ((), ())),
-        preferred_element_type=jnp.float32,
-        precision=lax.Precision.HIGHEST,
-    )
-    flat = jnp.sum(jnp.where(lax.shift_right_logical(lane, 4) == row16, placed, 0.0), axis=0, keepdims=True)
-    amount = jnp.broadcast_to(jnp.sum(live, axis=1, keepdims=True), (1, LANES))
+    amount = jnp.sum(jnp.sum(counts, axis=1, keepdims=True), axis=0, keepdims=True)
 
     def halves(value):
         high = jnp.floor(value * (1.0 / 256.0))
-        return high, value - high * 256.0
-
-    flat_high, flat_low = halves(flat)
-    rows = [flat_high[:, :LANES], flat_high[:, LANES:], flat_low[:, :LANES], flat_low[:, LANES:]]
-    rows += list(halves(amount)) + [jnp.zeros((2, LANES), jnp.float32)]
+        return [high, value - high * 256.0]
+
+    rows = halves(counts) + halves(jnp.broadcast_to(amount, (1, LANES))) + [jnp.zeros((6, LANES), jnp.float32)]
     for i in range(tiles):
         fetch(i).wait()
     lane = lax.shift_right_logical(lax.broadcasted_iota(jnp.int32, tile_ref.shape[1:], 1), 3)
@@ -100,9 +86,10 @@
 def prepare(group, anchor, energy, copies, groups):
     total = anchor.shape[0]
     components = energy.shape[0]
+    rows = components + 2 * groups * STATE_TILE // LANES + 8
     return pl.pallas_call(
         prepare_kernel,
-        out_shape=jax.ShapeDtypeStruct((copies, components + 8, LANES), jnp.bfloat16),
+        out_shape=jax.ShapeDtypeStruct((copies, rows, LANES), jnp.bfloat16),
         grid_spec=pltpu.PrefetchScalarGridSpec(
             num_scalar_prefetch=1,
             grid=(1,),
@@ -110,7 +97,7 @@
                 pl.BlockSpec((1, total), lambda i, g: (0, 0)),
                 pl.BlockSpec(memory_space=pltpu.HBM),
             ],
-            out_specs=pl.BlockSpec((copies, components + 8, LANES), lambda i, g: (0, 0, 0)),
+            out_specs=pl.BlockSpec((copies, rows, LANES), lambda i, g: (0, 0, 0)),
             scratch_shapes=[
                 pltpu.VMEM((groups, components, LANES), jnp.bfloat16),
                 pltpu.SemaphoreType.DMA((groups,)),
@@ -121,16 +108,18 @@
     )(group, anchor.reshape(1, total), energy)
 
 
-def arrange_kernel(group_ref, own_ref, pieces_ref, left_ref, amount_ref, wide_ref):
-    components = pieces_ref.shape[1] - 8
+def arrange_kernel(components, group_ref, own_ref, pieces_ref, left_ref, amount_ref, log_ref, wide_ref):
+    tall = log_ref.shape[0]
     wide_ref[...] = jnp.zeros_like(wide_ref)
     lane = lax.broadcasted_iota(jnp.int32, (1, LANES), 1)
     row = lax.broadcasted_iota(jnp.int32, (DEPTH - 3 * components, LANES), 0)
+    counts = jnp.zeros((tall, LANES), jnp.float32)
     at = jnp.int32(0)
     for b in range(pieces_ref.shape[0]):
         piece = pieces_ref[b].astype(jnp.float32)
         rest = piece[components:]
-        is_live = live_rows(group_ref[0], own_ref[0], rest[4:5] * 256.0 + rest[5:6])
+        counts += rest[:tall] * 256.0 + rest[tall : 2 * tall]
+        is_live = live_rows(group_ref[0], own_ref[0], rest[2 * tall : 2 * tall + 1] * 256.0 + rest[2 * tall + 1 : 2 * tall + 2])
         live = jnp.where(is_live, 1.0, 0.0)
         starts = jnp.where(lax.bitwise_and(lane, 7) == 0, live, 0.0)
         energy = piece[:components] * live
@@ -140,46 +129,42 @@
         at = at + 8 * jnp.sum(starts).astype(jnp.int32)
     left_ref[...] = wide_ref[...].astype(jnp.bfloat16)
     amount_ref[0] = at
-
-
-def arrange(group, own, pieces):
+    log_ref[...] = jnp.log(counts)
+
+
+def arrange(group, own, pieces, components, groups):
     most = pl.cdiv(pieces.shape[0] * LANES, ROW_TILE) * ROW_TILE
     smem = pl.BlockSpec(memory_space=pltpu.SMEM)
     vmem = pl.BlockSpec(memory_space=pltpu.VMEM)
     return pl.pallas_call(
-        arrange_kernel,
+        functools.partial(arrange_kernel, components),
         out_shape=[
             jax.ShapeDtypeStruct((most, DEPTH), jnp.bfloat16),
             jax.ShapeDtypeStruct((1,), jnp.int32),
+            jax.ShapeDtypeStruct((groups * STATE_TILE // LANES, LANES), jnp.float32),
         ],
         in_specs=[smem, smem, vmem],
-        out_specs=[vmem, smem],
+        out_specs=[vmem, smem, vmem],
         scratch_shapes=[pltpu.VMEM((most, DEPTH), jnp.float32)],
         compiler_params=pltpu.CompilerParams(vmem_limit_bytes=6 * 2**20),
         name="arrange",
     )(group, own, pieces)
 
 
-def pack_kernel(pieces_ref, start_ref, coef_ref, out_ref):
-    components = coef_ref.shape[0]
-    counts = jnp.sum(pieces_ref[:, components:, :].astype(jnp.float32), axis=0)
-    counts = jnp.concatenate([counts[0:1], counts[1:2]], axis=1) * 256.0 + jnp.concatenate(
-        [counts[2:3], counts[3:4]], axis=1
-    )
-    rows = list(split3(jnp.log(counts))) + list(split3(start_ref[...]))
-    rows.append(jnp.zeros((2, STATE_TILE), jnp.float32))
+def pack_kernel(start_ref, coef_ref, out_ref):
+    rows = list(split3(start_ref[...])) + [jnp.zeros((5, STATE_TILE), jnp.float32)]
     packed = jnp.concatenate([coef_ref[...].astype(jnp.float32)] + rows, axis=0).astype(jnp.bfloat16)
     out_ref[...] = jnp.broadcast_to(packed[None], out_ref.shape)
 
 
-def pack(pieces, f_start, coef, copies):
+def pack(f_start, coef, copies):
     components, states = coef.shape
     return pl.pallas_call(
         pack_kernel,
         out_shape=jax.ShapeDtypeStruct((copies, components + 8, states), jnp.bfloat16),
         compiler_params=pltpu.CompilerParams(vmem_limit_bytes=4 * 2**20),
         name="pack",
-    )(pieces, f_start.reshape(1, states), coef)
+    )(f_start.reshape(1, states), coef)
 
 
 def merge_logs(parts):
@@ -215,10 +200,10 @@
 
 def sweep_kernel(first, *refs):
     if first:
-        amount_ref, packed_ref, left_ref, part_ref, wide_ref, shifted_ref, right_ref, scaled_ref, acc_ref, some_ref, tall_ref, top_ref = refs
+        amount_ref, packed_ref, log_ref, left_ref, part_ref, wide_ref, shifted_ref, right_ref, scaled_ref, acc_ref, some_ref, tall_ref, top_ref = refs
         source_ref = shifted_ref
     else:
-        amount_ref, packed_ref, left_ref, parts_ref, old_ref, part_ref, wide_ref, some_ref, right_ref, scaled_ref, acc_ref, tall_ref, top_ref = refs
+        amount_ref, packed_ref, log_ref, left_ref, parts_ref, old_ref, part_ref, wide_ref, some_ref, right_ref, scaled_ref, acc_ref, tall_ref, top_ref = refs
         source_ref = left_ref
     groups, packed_rows, _ = packed_ref.shape
     components = packed_rows - 8
@@ -227,17 +212,17 @@
     amount = amount_ref[0]
     tiles = (amount + ROW_TILE - 1) // ROW_TILE
 
-    for g in range(groups):
-        rows = packed_ref[g, components:, :].astype(jnp.float32)
-        log_counts = rows[0:1] + rows[1:2] + rows[2:3]
-        value = log_counts + (rows[3:4] + rows[4:5] + rows[5:6]) if first else log_counts
-        for h in range(pair):
-            wide_ref[pair * g + h : pair * g + h + 1, :] = value[:, h * LANES : (h + 1) * LANES]
     if first:
-        weights = wide_ref[...]
+        for g in range(groups):
+            rows = packed_ref[g, components : components + 3, :].astype(jnp.float32)
+            start = rows[0:1] + rows[1:2] + rows[2:3]
+            for h in range(pair):
+                wide_ref[pair * g + h : pair * g + h + 1, :] = start[:, h * LANES : (h + 1) * LANES]
+        weights = wide_ref[...] + log_ref[...]
+        wide_ref[...] = weights
     else:
         raw = old_ref[...] - merge_logs(parts_ref[...]) * LN2
-        wide = wide_ref[...] + centered(raw)
+        wide = log_ref[...] + centered(raw)
         wide_ref[...] = wide
         weights = wide - largest(wide - old_ref[...])
     w0, w1, w2 = split3(weights * LOG2E)
@@ -365,12 +350,12 @@
         give(top_ref[...] + jnp.log2(acc_ref[0:1, :]))
 
 
-def sweep(amount, packed, left, parts, old, copies):
+def sweep(amount, packed, log_counts, left, parts, old, copies):
     groups = packed.shape[0]
     states = groups * STATE_TILE
     first = parts is None
     tall = states // LANES
-    operands = [amount, packed, left] + ([] if first else [parts, old])
+    operands = [amount, packed, log_counts, left] + ([] if first else [parts, old])
     outs = [((copies, tall, LANES), jnp.float32), ((tall, LANES), jnp.float32)]
     scratch = [
         pltpu.VMEM((DEPTH, states), jnp.bfloat16),
@@ -429,13 +414,15 @@
     blocks = lax.axis_size("sample")
     group = lax.axis_index("state").astype(jnp.int32).reshape(1)
     own = lax.axis_index("sample").astype(jnp.int32).reshape(1)
-    pieces = spread(prepare(group, anchor, energy, blocks, groups), "sample")
-    packed = spread(pack(pieces, f_start, coef, groups), "state")
-    left, amount = arrange(group, own, pieces)
+    packed = spread(pack(f_start, coef, groups), "state")
+    prepared = prepare(group, anchor, energy, blocks, groups)
+    prepared, packed = lax.optimization_barrier((prepared, packed))
+    pieces = spread(prepared, "sample")
+    left, amount, log_counts = arrange(group, own, pieces, energy.shape[0], groups)
     parts = None
     weights = None
     for iteration in range(ITERS):
-        part, weights, *rest = sweep(amount, packed, left, parts, weights, blocks)
+        part, weights, *rest = sweep(amount, packed, log_counts, left, parts, weights, blocks)
         if rest:
             left = rest[0]
         parts = spread(merge(spread(part, "sample"), groups), "state")

time: 139 us -> 143 us (1.029)
  blocking collectives: 74 us -> 52.9 us
  starting transfers between devices: 6.75 us -> 18.4 us
  waiting for transfers between devices: 7.73 us -> 17.6 us
  Pallas kernels: 49.7 us -> 51.9 us
    all_to_all x5 -> x4, blocking collectives: 74 us -> 52.9 us  [spread(): return lax.all_to_all(copies, axis, 0, 0)]
    all_to_all x1 -> x2, starting transfers between devices: 6.75 us -> 18.4 us  [spread(): return lax.all_to_all(copies, axis, 0, 0)]
    all_to_all x1 -> x2, waiting for transfers between devices: 7.73 us -> 17.6 us  [spread(): return lax.all_to_all(copies, axis, 0, 0)]
    pallas_call x2, Pallas kernels: 4.05 us -> 6.28 us  [the longest x1 5.42 us: prepare(): pl.pallas_call(prepare_kernel, out_shape=jax.ShapeDtypeStruct((copies, ro...]
  transfers between devices with their start and end apart: 1 -> 2, of which waited for: 1 -> 2; matrix products, arithmetic and copies ran while one was open for 0% -> 0% of each run, Pallas kernels for 1% -> 4%
where the time goes in v5:
time: 143 us; the launch traced here: 142 us
  blocking collectives  52.9 us (37%)
  Pallas kernels  51.9 us (36%)
  starting transfers between devices  18.4 us (13%)
  waiting for transfers between devices  17.6 us (12%)
    all_to_all x4, blocking collectives, spread(): return lax.all_to_all(copies, axis, 0, 0)  52.9 us
    pallas_call x2, Pallas kernels, sweep(): pl.pallas_call(functools.partial(sweep_kernel, first), out_shape=[jax.Sha...  44 us
    all_to_all x2, starting transfers between devices, spread(): return lax.all_to_all(copies, axis, 0, 0)  18.4 us
    all_to_all x2, waiting for transfers between devices, spread(): return lax.all_to_all(copies, axis, 0, 0)  17.6 us
    pallas_call x1, Pallas kernels, prepare(): pl.pallas_call(prepare_kernel, out_shape=jax.ShapeDtypeStruct((copies, ro...  5.42 us
  transfers between devices with their start and end apart: 2, of which 2 were waited for; matrix products, arithmetic and copies ran while one was open for 0% of the time, Pallas kernels for 4%

profile of v5, /device:TPU:1, one launch (start us, length us, event | category | flops | bytes accessed | tf_op | source)
XLA Modules:
  0.0 142.3 jit_solution(3116319314020240126)
XLA Ops:
  0.0 0.0 copy-start
  0.0 0.7 copy-done
  0.7 0.0 copy-start.1
  0.7 0.7 copy-done.1
  1.4 0.8 pack.1
  2.2 7.6 %all-to-all-start = ((bf16[16,40,256]{2,1,0:T(8,128)(2,1)}), bf16[16,40,256]{2,1,0:T(8,128)(2,1)S(1)}, u32[]{:S(2)}, u32[]{:S(2)}) async-start(bf16[16,40,256]{2,1,0:T(8,128)(2,1)} %pack.1), calls=%async_computation | async-start | bytes 655360 | tf_op jit(solution)/shard_map/all_to_all | solution.py:409
  9.8 5.4 %prepare.1 = bf16[16,104,128]{2,1,0:T(8,128)(2,1)} custom-call(s32[1]{0:T(128)} %bitcast.group_ref, s32[1,32768]{1,0:T(1,128)} %bitcast.6, bf16[32,32768]{1,0:T(8,128)(2,1)} %energy_ref.1), custom_call_target="tpu_custom_call" | custom-call | tf_op jit(solution)/shard_map/prepare/pallas_call | solution.py:90
  15.2 2.4 %all-to-all-done.refs_1_ = bf16[16,40,256]{2,1,0:T(8,128)(2,1)S(1)} async-done(((bf16[16,40,256]{2,1,0:T(8,128)(2,1)}), bf16[16,40,256]{2,1,0:T(8,128)(2,1)S(1)}, u32[]{:S(2)}, u32[]{:S(2)}) %all-to-all-start) | async-done | bytes 327712 | tf_op jit(solution)/shard_map/all_to_all | solution.py:409
  17.6 10.8 %all-to-all-start.1 = ((bf16[16,104,128]{2,1,0:T(8,128)(2,1)}), bf16[16,104,128]{2,1,0:T(8,128)(2,1)S(1)}, u32[]{:S(2)}, u32[]{:S(2)}) async-start(bf16[16,104,128]{2,1,0:T(8,128)(2,1)} %prepare.1), calls=%async_computation.1 | async-start | bytes 851968 | tf_op jit(solution)/shard_map/all_to_all | solution.py:409
  28.4 15.2 %all-to-all-done.1.pieces_ref = bf16[16,104,128]{2,1,0:T(8,128)(2,1)S(1)} async-done(((bf16[16,104,128]{2,1,0:T(8,128)(2,1)}), bf16[16,104,128]{2,1,0:T(8,128)(2,1)S(1)}, u32[]{:S(2)}, u32[]{:S(2)}) %all-to-all-start.1) | async-done | bytes 426016 | tf_op jit(solution)/shard_map/all_to_all | solution.py:409
  43.6 0.9 arrange.1
  44.5 39.0 %first_sweep.1 = (f32[16,32,128]{2,1,0:T(8,128)S(1)}, f32[32,128]{1,0:T(8,128)S(1)}, bf16[2080,128]{1,0:T(8,128)(2,1)S(1)}) custom-call(s32[1]{0:T(128)} %get-tuple-element.16.refs_0_, bf16[16,40,256]{2,1,0:T(8,128)(2,1)S(1)} %all-to-all-done.refs_1_, f32[32,128]{1,0:T(8,128)S(1)} %get-tuple-element.18.refs_2_, bf16[2080,128]{1,0:T(8,128)(2,1)S(1)} %get-tuple-element.19.refs_3_), custom_call_target="tpu_custom_call" | custom-call | tf_op jit(solution)/shard_map/first_sweep/pallas_call | solution.py:372
  83.5 14.4 %all_to_all.30.parts_ref = f32[16,32,128]{2,1,0:T(8,128)S(1)} all-to-all(f32[16,32,128]{2,1,0:T(8,128)S(1)} %get-tuple-element.21), channel_id=1, replica_groups=mesh['state'=16,'sample'=16] {'sample'}, dimensions={0} | all-to-all | bytes 524288 | tf_op jit(solution)/shard_map/all_to_all | solution.py:409
  97.9 0.1 merge.2
  97.9 11.2 %all_to_all.31.refs_4_ = f32[16,32,128]{2,1,0:T(8,128)S(1)} all-to-all(f32[16,32,128]{2,1,0:T(8,128)S(1)} %merge.2), channel_id=1, replica_groups=mesh['state'=16,'sample'=16] {'state'}, dimensions={0} | all-to-all | bytes 524288 | tf_op jit(solution)/shard_map/all_to_all | solution.py:409
  109.1 5.0 %next_sweep.1 = (f32[16,32,128]{2,1,0:T(8,128)S(1)}, f32[32,128]{1,0:T(8,128)S(1)}) custom-call(s32[1]{0:T(128)} %get-tuple-element.16.refs_0_, bf16[16,40,256]{2,1,0:T(8,128)(2,1)S(1)} %all-to-all-done.refs_1_, f32[32,128]{1,0:T(8,128)S(1)} %get-tuple-element.18.refs_2_, bf16[2080,128]{1,0:T(8,128)(2,1)S(1)} %get-tuple-element.20.refs_3_, ...), custom_call_target="tpu_custom_call" | custom-call | tf_op jit(solution)/shard_map/next_sweep/pallas_call | solution.py:372
  114.1 15.7 %all_to_all.32.parts_ref = f32[16,32,128]{2,1,0:T(8,128)S(1)} all-to-all(f32[16,32,128]{2,1,0:T(8,128)S(1)} %get-tuple-element.23), channel_id=1, replica_groups=mesh['state'=16,'sample'=16] {'sample'}, dimensions={0} | all-to-all | bytes 524288 | tf_op jit(solution)/shard_map/all_to_all | solution.py:409
  129.8 0.1 merge.3
  129.9 11.7 %all_to_all.33.parts_ref = f32[16,32,128]{2,1,0:T(8,128)S(1)} all-to-all(f32[16,32,128]{2,1,0:T(8,128)S(1)} %merge.3), channel_id=1, replica_groups=mesh['state'=16,'sample'=16] {'state'}, dimensions={0} | all-to-all | bytes 524288 | tf_op jit(solution)/shard_map/all_to_all | solution.py:409
  141.6 0.7 finish.1
Async XLA Ops:
  0.0 0.7 copy-start
  0.7 0.7 copy-start.1
  2.2 15.4 %all-to-all-start = ((bf16[16,40,256]{2,1,0:T(8,128)(2,1)}), bf16[16,40,256]{2,1,0:T(8,128)(2,1)S(1)}, u32[]{:S(2)}, u32[]{:S(2)}) async-start(bf16[16,40,256]{2,1,0:T(8,128)(2,1)} %pack.1), calls=%async_computation | async-start | bytes 655360 | tf_op jit(solution)/shard_map/all_to_all | solution.py:409
  17.6 26.0 %all-to-all-start.1 = ((bf16[16,104,128]{2,1,0:T(8,128)(2,1)}), bf16[16,104,128]{2,1,0:T(8,128)(2,1)S(1)}, u32[]{:S(2)}, u32[]{:S(2)}) async-start(bf16[16,104,128]{2,1,0:T(8,128)(2,1)} %prepare.1), calls=%async_computation.1 | async-start | bytes 851968 | tf_op jit(solution)/shard_map/all_to_all | solution.py:409

commit v6 on v4

--- a/solution.py
+++ b/solution.py
@@ -187,6 +187,23 @@
     return highest + jnp.log2(jnp.sum(jnp.exp2(parts - highest[None]), axis=0))
 
 
+def merge_pair_kernel(kept_ref, other_ref, out_ref):
+    kept = kept_ref[...]
+    other = other_ref[...]
+    highest = jnp.maximum(kept, other)
+    value = highest + jnp.log2(jnp.exp2(kept - highest) + jnp.exp2(other - highest))
+    out_ref[...] = jnp.broadcast_to(value[None], out_ref.shape)
+
+
+def merge_pair(kept, other, copies):
+    return pl.pallas_call(
+        merge_pair_kernel,
+        out_shape=jax.ShapeDtypeStruct((copies,) + kept.shape, jnp.float32),
+        compiler_params=pltpu.CompilerParams(vmem_limit_bytes=4 * 2**20),
+        name="merge_pair",
+    )(kept, other)
+
+
 def merge_kernel(parts_ref, out_ref):
     out_ref[...] = jnp.broadcast_to(merge_logs(parts_ref[...])[None], out_ref.shape)
 
@@ -215,10 +232,10 @@
 
 def sweep_kernel(first, *refs):
     if first:
-        amount_ref, packed_ref, left_ref, part_ref, wide_ref, shifted_ref, right_ref, scaled_ref, acc_ref, some_ref, tall_ref, top_ref = refs
+        amount_ref, own_ref, packed_ref, left_ref, kept_ref, sent_ref, wide_ref, shifted_ref, right_ref, scaled_ref, acc_ref, some_ref, tall_ref, top_ref = refs
         source_ref = shifted_ref
     else:
-        amount_ref, packed_ref, left_ref, parts_ref, old_ref, part_ref, wide_ref, some_ref, right_ref, scaled_ref, acc_ref, tall_ref, top_ref = refs
+        amount_ref, own_ref, packed_ref, left_ref, parts_ref, old_ref, kept_ref, sent_ref, wide_ref, some_ref, right_ref, scaled_ref, acc_ref, tall_ref, top_ref = refs
         source_ref = left_ref
     groups, packed_rows, _ = packed_ref.shape
     components = packed_rows - 8
@@ -315,7 +332,10 @@
     def give(value):
         for k in range(states // LANES):
             tall_ref[k : k + 1, :] = value[:, k * LANES : (k + 1) * LANES]
-        part_ref[...] = jnp.broadcast_to(tall_ref[...][None], part_ref.shape)
+        half = kept_ref.shape[0]
+        core = lax.rem(own_ref[0], 2)
+        kept_ref[...] = tall_ref[pl.ds(pl.multiple_of(core * half, half), half), :]
+        sent_ref[...] = tall_ref[pl.ds(pl.multiple_of((1 - core) * half, half), half), :]
 
     give(logs)
     enough = jnp.logical_and(smallest >= SAFE_SUM, smallest * least >= SAFE_SUM)
@@ -365,13 +385,13 @@
         give(top_ref[...] + jnp.log2(acc_ref[0:1, :]))
 
 
-def sweep(amount, packed, left, parts, old, copies):
+def sweep(amount, own, packed, left, parts, old):
     groups = packed.shape[0]
     states = groups * STATE_TILE
     first = parts is None
     tall = states // LANES
-    operands = [amount, packed, left] + ([] if first else [parts, old])
-    outs = [((copies, tall, LANES), jnp.float32), ((tall, LANES), jnp.float32)]
+    operands = [amount, own, packed, left] + ([] if first else [parts, old])
+    outs = [((tall // 2, LANES), jnp.float32)] * 2 + [((tall, LANES), jnp.float32)]
     scratch = [
         pltpu.VMEM((DEPTH, states), jnp.bfloat16),
         pltpu.VMEM((ROW_TILE, states), jnp.float32),
@@ -387,7 +407,7 @@
     return pl.pallas_call(
         functools.partial(sweep_kernel, first),
         out_shape=[jax.ShapeDtypeStruct(*out) for out in outs],
-        in_specs=[pl.BlockSpec(memory_space=pltpu.SMEM)] + [pl.BlockSpec(memory_space=pltpu.VMEM)] * (len(operands) - 1),
+        in_specs=[pl.BlockSpec(memory_space=pltpu.SMEM)] * 2 + [pl.BlockSpec(memory_space=pltpu.VMEM)] * (len(operands) - 2),
         scratch_shapes=scratch,
         compiler_params=pltpu.CompilerParams(vmem_limit_bytes=20 * 2**20),
         name="first_sweep" if first else "next_sweep",
@@ -420,8 +440,18 @@
     )(group, parts, old)
 
 
-def spread(copies, axis):
-    return lax.all_to_all(copies, axis, 0, 0)
+def spread(copies, axis, members=None):
+    return lax.all_to_all(copies, axis, 0, 0, axis_index_groups=members)
+
+
+def merged(kept, sent, groups, blocks):
+    chips = blocks // 2
+    other = lax.ppermute(sent, "sample", [(i, i ^ 1) for i in range(blocks)])
+    lines = [[2 * z + core for z in range(chips)] for core in range(2)]
+    along = spread(merge_pair(kept, other, chips), "sample", lines)
+    planes = [[blocks * s + 2 * z + core for s in range(groups) for core in range(2)] for z in range(chips)]
+    parts = spread(merge(along, 2 * groups), ("state", "sample"), planes)
+    return parts.reshape(groups, 2 * kept.shape[0], LANES)
 
 
 def per_device(energy, coef, anchor, f_start):
@@ -435,10 +465,10 @@
     parts = None
     weights = None
     for iteration in range(ITERS):
-        part, weights, *rest = sweep(amount, packed, left, parts, weights, blocks)
+        kept, sent, weights, *rest = sweep(amount, own, packed, left, parts, weights)
         if rest:
             left = rest[0]
-        parts = spread(merge(spread(part, "sample"), groups), "state")
+        parts = merged(kept, sent, groups, blocks)
     return finish(group, parts, weights).reshape(-1)
 
 

time: 139 us -> 135 us (0.971)
  blocking collectives: 74 us -> 66.4 us
  starting transfers between devices: 6.75 us -> 8.62 us
  waiting for transfers between devices: 7.73 us -> 9.55 us
    all_to_all x5, blocking collectives: 74 us -> 66.4 us  [spread(): return lax.all_to_all(copies, axis, 0, 0, axis_index_groups=members)]
    ppermute x0 -> x2, starting transfers between devices: none -> 1.87 us  [merged(): other = lax.ppermute(sent, 'sample', [(i, i ^ 1) for i in range(blocks)])]
    ppermute x0 -> x2, waiting for transfers between devices: none -> 1.81 us  [merged(): other = lax.ppermute(sent, 'sample', [(i, i ^ 1) for i in range(blocks)])]
  transfers between devices with their start and end apart: 1 -> 3, of which waited for: 1 -> 3; matrix products, arithmetic and copies ran while one was open for 0% -> 0% of each run, Pallas kernels for 1% -> 1%
where the time goes in v6:
time: 135 us; the launch traced here: 134 us
  blocking collectives  66.4 us (49%)
  Pallas kernels  49.5 us (37%)
  waiting for transfers between devices  9.55 us (7%)
  starting transfers between devices  8.62 us (6%)
    all_to_all x5, blocking collectives, spread(): return lax.all_to_all(copies, axis, 0, 0, axis_index_groups=members)  66.4 us
    pallas_call x2, Pallas kernels, sweep(): pl.pallas_call(functools.partial(sweep_kernel, first), out_shape=[jax.Sha...  43.9 us
    all_to_all x1, waiting for transfers between devices, spread(): return lax.all_to_all(copies, axis, 0, 0, axis_index_groups=members)  7.73 us
    all_to_all x1, starting transfers between devices, spread(): return lax.all_to_all(copies, axis, 0, 0, axis_index_groups=members)  6.75 us
    pallas_call x1, Pallas kernels, prepare(): pl.pallas_call(prepare_kernel, out_shape=jax.ShapeDtypeStruct((copies, co...  3.18 us
  transfers between devices with their start and end apart: 3, of which 3 were waited for; matrix products, arithmetic and copies ran while one was open for 0% of the time, Pallas kernels for 1%

profile of v6, /device:TPU:1, one launch (start us, length us, event | category | flops | bytes accessed | tf_op | source)
XLA Modules:
  0.0 134.2 jit_solution(1951112654708589836)
XLA Ops:
  0.0 0.0 copy-start.1
  0.0 0.0 copy-start
  0.0 3.2 %prepare.1 = bf16[16,40,128]{2,1,0:T(8,128)(2,1)} custom-call(s32[1]{0:T(128)} %bitcast.group_ref, s32[1,32768]{1,0:T(1,128)} %bitcast.10, bf16[32,32768]{1,0:T(8,128)(2,1)} %energy_ref.1), custom_call_target="tpu_custom_call" | custom-call | tf_op jit(solution)/shard_map/prepare/pallas_call | solution.py:103
  3.2 19.6 %all_to_all.30.pieces_ref = bf16[16,40,128]{2,1,0:T(8,128)(2,1)S(1)} all-to-all(bf16[16,40,128]{2,1,0:T(8,128)(2,1)} %prepare.1), channel_id=1, replica_groups=mesh['state'=16,'sample'=16] {'sample'}, dimensions={0} | all-to-all | bytes 327680 | tf_op jit(solution)/shard_map/all_to_all | solution.py:444
  22.8 0.0 copy-done.1
  22.8 0.0 copy-done
  22.8 0.8 pack.1
  23.6 6.8 %all-to-all-start.1 = ((bf16[16,40,256]{2,1,0:T(8,128)(2,1)}), bf16[16,40,256]{2,1,0:T(8,128)(2,1)S(1)}, u32[]{:S(2)}, u32[]{:S(2)}) async-start(bf16[16,40,256]{2,1,0:T(8,128)(2,1)} %pack.1), calls=%async_computation.1 | async-start | bytes 655360 | tf_op jit(solution)/shard_map/all_to_all | solution.py:444
  30.4 0.9 arrange.1
  31.2 7.7 %all-to-all-done.1.refs_2_ = bf16[16,40,256]{2,1,0:T(8,128)(2,1)S(1)} async-done(((bf16[16,40,256]{2,1,0:T(8,128)(2,1)}), bf16[16,40,256]{2,1,0:T(8,128)(2,1)S(1)}, u32[]{:S(2)}, u32[]{:S(2)}) %all-to-all-start.1) | async-done | bytes 327712 | tf_op jit(solution)/shard_map/all_to_all | solution.py:444
  39.0 38.9 %first_sweep.1 = (f32[16,128]{1,0:T(8,128)S(1)}, f32[16,128]{1,0:T(8,128)S(1)}, f32[32,128]{1,0:T(8,128)S(1)}, bf16[2080,128]{1,0:T(8,128)(2,1)S(1)}) custom-call(s32[1]{0:T(128)} %get-tuple-element.14.refs_0_, s32[1]{0:T(128)} %bitcast.1.own_ref.refs_1_, bf16[16,40,256]{2,1,0:T(8,128)(2,1)S(1)} %all-to-all-done.1.refs_2_, ...), custom_call_target="tpu_custom_call" | custom-call | tf_op jit(solution)/shard_map/first_sweep/pallas_call | solution.py:407
  77.9 1.6 %collective-permute-start = (f32[16,128]{1,0:T(8,128)S(1)}, f32[16,128]{1,0:T(8,128)S(1)}, u32[]{:S(2)}, u32[]{:S(2)}) collective-permute-start(f32[16,128]{1,0:T(8,128)S(1)} %get-tuple-element.18), channel_id=1, source_target_pairs={{0,1},{1,0},{2,3},{3,2},{4,5},{5,4},{6,7},{7,6},{8,9},{9,8},{10,11... | collective-permute-start | bytes 24584 | tf_op jit(solution)/shard_map/ppermute | solution.py:449
  79.5 0.8 collective-permute-done.other_ref
  80.4 9.5 %all_to_all.31.parts_ref = f32[8,16,128]{2,1,0:T(8,128)S(1)} all-to-all(f32[8,16,128]{2,1,0:T(8,128)S(1)} %merge_pair.2), channel_id=1, replica_groups={{0,2,4,6,8,10,12,14},{1,3,5,7,9,11,13,15},{16,18,20,22,24,26,28,30},{17..., dimensions={0} | all-to-all | bytes 131072 | tf_op jit(solution)/shard_map/all_to_all | solution.py:444
  89.9 14.1 %all_to_all.32 = f32[32,16,128]{2,1,0:T(8,128)S(1)} all-to-all(f32[32,16,128]{2,1,0:T(8,128)S(1)} %merge.2), channel_id=1, replica_groups={{0,1,16,17,32,33,48,49,64,65,80,81,96,97,112,113,128,129,144,145,160,16..., dimensions={0} | all-to-all | bytes 524288 | tf_op jit(solution)/shard_map/all_to_all | solution.py:444
  104.0 5.0 %next_sweep.1 = (f32[16,128]{1,0:T(8,128)S(1)}, f32[16,128]{1,0:T(8,128)S(1)}, f32[32,128]{1,0:T(8,128)S(1)}) custom-call(s32[1]{0:T(128)} %get-tuple-element.14.refs_0_, s32[1]{0:T(128)} %bitcast.1.own_ref.refs_1_, bf16[16,40,256]{2,1,0:T(8,128)(2,1)S(1)} %all-to-all-done.1.refs_2_, bf16[2080,128]{1,0:T(8,128)(2,1)S(1)} %get-tuple-element.16.refs_3_, ...), custom_call_target="tpu_custom_call" | custom-call | tf_op jit(solution)/shard_map/next_sweep/pallas_call | solution.py:407
  109.0 0.3 collective-permute-start.1
  109.2 1.0 collective-permute-done.1.other_ref
  110.2 9.5 %all_to_all.33.parts_ref = f32[8,16,128]{2,1,0:T(8,128)S(1)} all-to-all(f32[8,16,128]{2,1,0:T(8,128)S(1)} %merge_pair.3), channel_id=1, replica_groups={{0,2,4,6,8,10,12,14},{1,3,5,7,9,11,13,15},{16,18,20,22,24,26,28,30},{17..., dimensions={0} | all-to-all | bytes 131072 | tf_op jit(solution)/shard_map/all_to_all | solution.py:444
  119.8 13.7 %all_to_all.34 = f32[32,16,128]{2,1,0:T(8,128)S(1)} all-to-all(f32[32,16,128]{2,1,0:T(8,128)S(1)} %merge.3), channel_id=1, replica_groups={{0,1,16,17,32,33,48,49,64,65,80,81,96,97,112,113,128,129,144,145,160,16..., dimensions={0} | all-to-all | bytes 524288 | tf_op jit(solution)/shard_map/all_to_all | solution.py:444
  133.5 0.7 finish.1
  (4 shorter events, 0.1 us)
Async XLA Ops:
  0.0 22.8 %copy-start.1 = (f32[256]{0:T(256)S(1)}, f32[256]{0:T(256)}, u32[]{:S(2)}) copy-start(f32[256]{0:T(256)} %param.7) | copy-start | bytes 3076
  0.0 22.8 %copy-start = (bf16[32,256]{1,0:T(8,128)(2,1)S(1)}, bf16[32,256]{1,0:T(8,128)(2,1)}, u32[]{:S(2)}) copy-start(bf16[32,256]{1,0:T(8,128)(2,1)} %coef_ref.1) | copy-start | bytes 49156
  23.6 15.4 %all-to-all-start.1 = ((bf16[16,40,256]{2,1,0:T(8,128)(2,1)}), bf16[16,40,256]{2,1,0:T(8,128)(2,1)S(1)}, u32[]{:S(2)}, u32[]{:S(2)}) async-start(bf16[16,40,256]{2,1,0:T(8,128)(2,1)} %pack.1), calls=%async_computation.1 | async-start | bytes 655360 | tf_op jit(solution)/shard_map/all_to_all | solution.py:444
  77.9 2.4 %collective-permute-start = (f32[16,128]{1,0:T(8,128)S(1)}, f32[16,128]{1,0:T(8,128)S(1)}, u32[]{:S(2)}, u32[]{:S(2)}) collective-permute-start(f32[16,128]{1,0:T(8,128)S(1)} %get-tuple-element.18), channel_id=1, source_target_pairs={{0,1},{1,0},{2,3},{3,2},{4,5},{5,4},{6,7},{7,6},{8,9},{9,8},{10,11... | collective-permute-start | bytes 24584 | tf_op jit(solution)/shard_map/ppermute | solution.py:449
  109.0 1.3 collective-permute-start.1

commit v7 on v6

--- a/solution.py
+++ b/solution.py
@@ -39,7 +39,7 @@
     return slot.astype(jnp.float32) < live_slots
 
 
-def prepare_kernel(group_ref, anchor_ref, energy_ref, out_ref, tile_ref, sems):
+def prepare_kernel(group_ref, anchor_hbm_ref, energy_ref, out_ref, anchor_ref, tile_ref, anchor_sems, sems):
     group = group_ref[0]
     tiles = tile_ref.shape[0]
 
@@ -47,15 +47,23 @@
         at = pl.multiple_of((group + tiles * i) * LANES, LANES)
         return pltpu.make_async_copy(energy_ref.at[:, pl.ds(at, LANES)], tile_ref.at[i], sems.at[i])
 
+    total = anchor_ref.shape[1]
+    step = 4096
+
+    def fetch_anchor(k):
+        part = pl.ds(k * step, step)
+        return pltpu.make_async_copy(anchor_hbm_ref.at[:, part], anchor_ref.at[:, part], anchor_sems.at[k])
+
+    for k in range(total // step):
+        fetch_anchor(k).start()
     for i in range(tiles):
         fetch(i).start()
     base = group * 16
-    total = anchor_ref.shape[1]
-    step = 4096
     row = lax.broadcasted_iota(jnp.int32, (16, step), 0)
     counts = jnp.zeros((16, 16), jnp.float32)
     live = jnp.zeros((1, step), jnp.float32)
     for start in range(0, total, step):
+        fetch_anchor(start // step).wait()
         anchor = anchor_ref[:, start : start + step]
         high = lax.shift_right_logical(anchor, 4) - base
         low = lax.bitwise_and(anchor, 15)
@@ -100,25 +108,25 @@
 def prepare(group, anchor, energy, copies, groups):
     total = anchor.shape[0]
     components = energy.shape[0]
+    hbm = pltpu.MemorySpace.HBM
     return pl.pallas_call(
         prepare_kernel,
         out_shape=jax.ShapeDtypeStruct((copies, components + 8, LANES), jnp.bfloat16),
-        grid_spec=pltpu.PrefetchScalarGridSpec(
-            num_scalar_prefetch=1,
-            grid=(1,),
-            in_specs=[
-                pl.BlockSpec((1, total), lambda i, g: (0, 0)),
-                pl.BlockSpec(memory_space=pltpu.HBM),
-            ],
-            out_specs=pl.BlockSpec((copies, components + 8, LANES), lambda i, g: (0, 0, 0)),
-            scratch_shapes=[
-                pltpu.VMEM((groups, components, LANES), jnp.bfloat16),
-                pltpu.SemaphoreType.DMA((groups,)),
-            ],
-        ),
-        compiler_params=pltpu.CompilerParams(vmem_limit_bytes=56 * 2**20),
+        in_specs=[pl.BlockSpec(memory_space=pltpu.SMEM)] + [pl.BlockSpec(memory_space=hbm)] * 2,
+        out_specs=pl.BlockSpec(memory_space=pltpu.VMEM),
+        scratch_shapes=[
+            pltpu.VMEM((1, total), jnp.int32),
+            pltpu.VMEM((groups, components, LANES), jnp.bfloat16),
+            pltpu.SemaphoreType.DMA((total // 4096,)),
+            pltpu.SemaphoreType.DMA((groups,)),
+        ],
+        compiler_params=pltpu.CompilerParams(vmem_limit_bytes=8 * 2**20),
         name="prepare",
-    )(group, anchor.reshape(1, total), energy)
+    )(
+        group,
+        pltpu.with_memory_space_constraint(anchor.reshape(1, total), hbm),
+        pltpu.with_memory_space_constraint(energy, hbm),
+    )
 
 
 def arrange_kernel(group_ref, own_ref, pieces_ref, left_ref, amount_ref, wide_ref):

time: 135 us -> 134 us (level)
  no operation moved by 1% of the time
where the time goes in v7:
time: 134 us
  blocking collectives  66.3 us (49%)
  Pallas kernels  49.3 us (37%)
  waiting for transfers between devices  9.55 us (7%)
  starting transfers between devices  8.62 us (6%)
    all_to_all x5, blocking collectives, spread(): return lax.all_to_all(copies, axis, 0, 0, axis_index_groups=members)  66.3 us
    pallas_call x2, Pallas kernels, sweep(): pl.pallas_call(functools.partial(sweep_kernel, first), out_shape=[jax.Sha...  43.9 us
    all_to_all x1, waiting for transfers between devices, spread(): return lax.all_to_all(copies, axis, 0, 0, axis_index_groups=members)  7.73 us
    all_to_all x1, starting transfers between devices, spread(): return lax.all_to_all(copies, axis, 0, 0, axis_index_groups=members)  6.75 us
    pallas_call x1, Pallas kernels, prepare(): pl.pallas_call(prepare_kernel, out_shape=jax.ShapeDtypeStruct((copies, co...  2.95 us
  transfers between devices with their start and end apart: 3, of which 3 were waited for; matrix products, arithmetic and copies ran while one was open for 0% of the time, Pallas kernels for 1%

profile of v7, /device:TPU:1, one launch (start us, length us, event | category | flops | bytes accessed | tf_op | source)
XLA Modules:
  0.0 133.8 jit_solution(12405915713282430314)
XLA Ops:
  0.0 0.0 copy-start.1
  0.0 0.0 copy-start
  0.0 3.0 %prepare.1 = bf16[16,40,128]{2,1,0:T(8,128)(2,1)S(1)} custom-call(s32[1]{0:T(128)} %bitcast.group_ref, s32[1,32768]{1,0:T(1,128)} %bitcast.10, bf16[32,32768]{1,0:T(8,128)(2,1)} %energy_ref.1), custom_call_target="tpu_custom_call" | custom-call | tf_op jit(solution)/shard_map/prepare/pallas_call | solution.py:112
  3.0 19.4 %all_to_all.30.pieces_ref = bf16[16,40,128]{2,1,0:T(8,128)(2,1)S(1)} all-to-all(bf16[16,40,128]{2,1,0:T(8,128)(2,1)S(1)} %prepare.1), channel_id=1, replica_groups=mesh['state'=16,'sample'=16] {'sample'}, dimensions={0} | all-to-all | bytes 327680 | tf_op jit(solution)/shard_map/all_to_all | solution.py:452
  22.4 0.0 copy-done.1
  22.4 0.0 copy-done
  22.4 0.8 pack.1
  23.2 6.8 %all-to-all-start.1 = ((bf16[16,40,256]{2,1,0:T(8,128)(2,1)}), bf16[16,40,256]{2,1,0:T(8,128)(2,1)S(1)}, u32[]{:S(2)}, u32[]{:S(2)}) async-start(bf16[16,40,256]{2,1,0:T(8,128)(2,1)} %pack.1), calls=%async_computation.1 | async-start | bytes 655360 | tf_op jit(solution)/shard_map/all_to_all | solution.py:452
  29.9 0.9 arrange.1
  30.8 7.7 %all-to-all-done.1.refs_2_ = bf16[16,40,256]{2,1,0:T(8,128)(2,1)S(1)} async-done(((bf16[16,40,256]{2,1,0:T(8,128)(2,1)}), bf16[16,40,256]{2,1,0:T(8,128)(2,1)S(1)}, u32[]{:S(2)}, u32[]{:S(2)}) %all-to-all-start.1) | async-done | bytes 327712 | tf_op jit(solution)/shard_map/all_to_all | solution.py:452
  38.5 38.9 %first_sweep.1 = (f32[16,128]{1,0:T(8,128)S(1)}, f32[16,128]{1,0:T(8,128)S(1)}, f32[32,128]{1,0:T(8,128)S(1)}, bf16[2080,128]{1,0:T(8,128)(2,1)S(1)}) custom-call(s32[1]{0:T(128)} %get-tuple-element.14.refs_0_, s32[1]{0:T(128)} %bitcast.1.own_ref.refs_1_, bf16[16,40,256]{2,1,0:T(8,128)(2,1)S(1)} %all-to-all-done.1.refs_2_, ...), custom_call_target="tpu_custom_call" | custom-call | tf_op jit(solution)/shard_map/first_sweep/pallas_call | solution.py:415
  77.5 1.6 %collective-permute-start = (f32[16,128]{1,0:T(8,128)S(1)}, f32[16,128]{1,0:T(8,128)S(1)}, u32[]{:S(2)}, u32[]{:S(2)}) collective-permute-start(f32[16,128]{1,0:T(8,128)S(1)} %get-tuple-element.18), channel_id=1, source_target_pairs={{0,1},{1,0},{2,3},{3,2},{4,5},{5,4},{6,7},{7,6},{8,9},{9,8},{10,11... | collective-permute-start | bytes 24584 | tf_op jit(solution)/shard_map/ppermute | solution.py:457
  79.1 0.8 collective-permute-done.other_ref
  79.9 9.5 %all_to_all.31.parts_ref = f32[8,16,128]{2,1,0:T(8,128)S(1)} all-to-all(f32[8,16,128]{2,1,0:T(8,128)S(1)} %merge_pair.2), channel_id=1, replica_groups={{0,2,4,6,8,10,12,14},{1,3,5,7,9,11,13,15},{16,18,20,22,24,26,28,30},{17..., dimensions={0} | all-to-all | bytes 131072 | tf_op jit(solution)/shard_map/all_to_all | solution.py:452
  89.5 14.1 %all_to_all.32 = f32[32,16,128]{2,1,0:T(8,128)S(1)} all-to-all(f32[32,16,128]{2,1,0:T(8,128)S(1)} %merge.2), channel_id=1, replica_groups={{0,1,16,17,32,33,48,49,64,65,80,81,96,97,112,113,128,129,144,145,160,16..., dimensions={0} | all-to-all | bytes 524288 | tf_op jit(solution)/shard_map/all_to_all | solution.py:452
  103.6 5.0 %next_sweep.1 = (f32[16,128]{1,0:T(8,128)S(1)}, f32[16,128]{1,0:T(8,128)S(1)}, f32[32,128]{1,0:T(8,128)S(1)}) custom-call(s32[1]{0:T(128)} %get-tuple-element.14.refs_0_, s32[1]{0:T(128)} %bitcast.1.own_ref.refs_1_, bf16[16,40,256]{2,1,0:T(8,128)(2,1)S(1)} %all-to-all-done.1.refs_2_, bf16[2080,128]{1,0:T(8,128)(2,1)S(1)} %get-tuple-element.16.refs_3_, ...), custom_call_target="tpu_custom_call" | custom-call | tf_op jit(solution)/shard_map/next_sweep/pallas_call | solution.py:415
  108.5 0.3 collective-permute-start.1
  108.8 1.0 collective-permute-done.1.other_ref
  109.8 9.5 %all_to_all.33.parts_ref = f32[8,16,128]{2,1,0:T(8,128)S(1)} all-to-all(f32[8,16,128]{2,1,0:T(8,128)S(1)} %merge_pair.3), channel_id=1, replica_groups={{0,2,4,6,8,10,12,14},{1,3,5,7,9,11,13,15},{16,18,20,22,24,26,28,30},{17..., dimensions={0} | all-to-all | bytes 131072 | tf_op jit(solution)/shard_map/all_to_all | solution.py:452
  119.4 13.7 %all_to_all.34 = f32[32,16,128]{2,1,0:T(8,128)S(1)} all-to-all(f32[32,16,128]{2,1,0:T(8,128)S(1)} %merge.3), channel_id=1, replica_groups={{0,1,16,17,32,33,48,49,64,65,80,81,96,97,112,113,128,129,144,145,160,16..., dimensions={0} | all-to-all | bytes 524288 | tf_op jit(solution)/shard_map/all_to_all | solution.py:452
  133.1 0.7 finish.1
  (4 shorter events, 0.1 us)
Async XLA Ops:
  0.0 22.4 %copy-start.1 = (f32[256]{0:T(256)S(1)}, f32[256]{0:T(256)}, u32[]{:S(2)}) copy-start(f32[256]{0:T(256)} %param.7) | copy-start | bytes 3076
  0.0 22.4 %copy-start = (bf16[32,256]{1,0:T(8,128)(2,1)S(1)}, bf16[32,256]{1,0:T(8,128)(2,1)}, u32[]{:S(2)}) copy-start(bf16[32,256]{1,0:T(8,128)(2,1)} %coef_ref.1) | copy-start | bytes 49156
  23.2 15.4 %all-to-all-start.1 = ((bf16[16,40,256]{2,1,0:T(8,128)(2,1)}), bf16[16,40,256]{2,1,0:T(8,128)(2,1)S(1)}, u32[]{:S(2)}, u32[]{:S(2)}) async-start(bf16[16,40,256]{2,1,0:T(8,128)(2,1)} %pack.1), calls=%async_computation.1 | async-start | bytes 655360 | tf_op jit(solution)/shard_map/all_to_all | solution.py:452
  77.5 2.4 %collective-permute-start = (f32[16,128]{1,0:T(8,128)S(1)}, f32[16,128]{1,0:T(8,128)S(1)}, u32[]{:S(2)}, u32[]{:S(2)}) collective-permute-start(f32[16,128]{1,0:T(8,128)S(1)} %get-tuple-element.18), channel_id=1, source_target_pairs={{0,1},{1,0},{2,3},{3,2},{4,5},{5,4},{6,7},{7,6},{8,9},{9,8},{10,11... | collective-permute-start | bytes 24584 | tf_op jit(solution)/shard_map/ppermute | solution.py:457
  108.5 1.3 collective-permute-start.1

commit v8 on v7

--- a/solution.py
+++ b/solution.py
@@ -428,8 +428,8 @@
     out_ref[...] = hold_ref[pl.ds(group_ref[0] * out_ref.shape[0], out_ref.shape[0]), :]
 
 
-def finish(group, parts, old):
-    rows = old.shape[0] // parts.shape[0]
+def finish(group, parts, old, groups):
+    rows = old.shape[0] // groups
     return pl.pallas_call(
         finish_kernel,
         out_shape=jax.ShapeDtypeStruct((rows, LANES), jnp.float32),
@@ -448,18 +448,15 @@
     )(group, parts, old)
 
 
-def spread(copies, axis, members=None):
-    return lax.all_to_all(copies, axis, 0, 0, axis_index_groups=members)
+def spread(copies, axis):
+    return lax.all_to_all(copies, axis, 0, 0)
 
 
 def merged(kept, sent, groups, blocks):
-    chips = blocks // 2
     other = lax.ppermute(sent, "sample", [(i, i ^ 1) for i in range(blocks)])
-    lines = [[2 * z + core for z in range(chips)] for core in range(2)]
-    along = spread(merge_pair(kept, other, chips), "sample", lines)
-    planes = [[blocks * s + 2 * z + core for s in range(groups) for core in range(2)] for z in range(chips)]
-    parts = spread(merge(along, 2 * groups), ("state", "sample"), planes)
-    return parts.reshape(groups, 2 * kept.shape[0], LANES)
+    across = spread(merge_pair(kept, other, groups), "state")
+    parts = spread(merge(across, blocks), "sample")
+    return parts.reshape(blocks // 2, 2 * kept.shape[0], LANES)
 
 
 def per_device(energy, coef, anchor, f_start):
@@ -477,7 +474,7 @@
         if rest:
             left = rest[0]
         parts = merged(kept, sent, groups, blocks)
-    return finish(group, parts, weights).reshape(-1)
+    return finish(group, parts, weights, groups).reshape(-1)
 
 
 def solution(mesh):

time: 134 us -> 134 us (level)
  no operation moved by 1% of the time
where the time goes in v8:
time: 134 us; the launch traced here: 133 us
  blocking collectives  65.7 us (49%)
  Pallas kernels  49.3 us (37%)
  waiting for transfers between devices  9.72 us (7%)
  starting transfers between devices  8.43 us (6%)
    all_to_all x5, blocking collectives, spread(): return lax.all_to_all(copies, axis, 0, 0)  65.7 us
    pallas_call x2, Pallas kernels, sweep(): pl.pallas_call(functools.partial(sweep_kernel, first), out_shape=[jax.Sha...  43.8 us
    all_to_all x1, waiting for transfers between devices, spread(): return lax.all_to_all(copies, axis, 0, 0)  7.73 us
    all_to_all x1, starting transfers between devices, spread(): return lax.all_to_all(copies, axis, 0, 0)  6.75 us
    pallas_call x1, Pallas kernels, prepare(): pl.pallas_call(prepare_kernel, out_shape=jax.ShapeDtypeStruct((copies, co...  2.95 us
  transfers between devices with their start and end apart: 3, of which 3 were waited for; matrix products, arithmetic and copies ran while one was open for 0% of the time, Pallas kernels for 1%

profile of v8, /device:TPU:1, one launch (start us, length us, event | category | flops | bytes accessed | tf_op | source)
XLA Modules:
  0.0 133.2 jit_solution(7040492547193941479)
XLA Ops:
  0.0 0.0 copy-start.1
  0.0 0.0 copy-start
  0.0 3.0 %prepare.1 = bf16[16,40,128]{2,1,0:T(8,128)(2,1)S(1)} custom-call(s32[1]{0:T(128)} %bitcast.group_ref, s32[1,32768]{1,0:T(1,128)} %bitcast.10, bf16[32,32768]{1,0:T(8,128)(2,1)} %energy_ref.1), custom_call_target="tpu_custom_call" | custom-call | tf_op jit(solution)/shard_map/prepare/pallas_call | solution.py:112
  3.0 19.4 %all_to_all.30.pieces_ref = bf16[16,40,128]{2,1,0:T(8,128)(2,1)S(1)} all-to-all(bf16[16,40,128]{2,1,0:T(8,128)(2,1)S(1)} %prepare.1), channel_id=1, replica_groups=mesh['state'=16,'sample'=16] {'sample'}, dimensions={0} | all-to-all | bytes 327680 | tf_op jit(solution)/shard_map/all_to_all | solution.py:452
  22.4 0.0 copy-done.1
  22.4 0.0 copy-done
  22.4 0.8 pack.1
  23.2 6.8 %all-to-all-start.1 = ((bf16[16,40,256]{2,1,0:T(8,128)(2,1)}), bf16[16,40,256]{2,1,0:T(8,128)(2,1)S(1)}, u32[]{:S(2)}, u32[]{:S(2)}) async-start(bf16[16,40,256]{2,1,0:T(8,128)(2,1)} %pack.1), calls=%async_computation.1 | async-start | bytes 655360 | tf_op jit(solution)/shard_map/all_to_all | solution.py:452
  29.9 0.9 arrange.1
  30.8 7.7 %all-to-all-done.1.refs_2_ = bf16[16,40,256]{2,1,0:T(8,128)(2,1)S(1)} async-done(((bf16[16,40,256]{2,1,0:T(8,128)(2,1)}), bf16[16,40,256]{2,1,0:T(8,128)(2,1)S(1)}, u32[]{:S(2)}, u32[]{:S(2)}) %all-to-all-start.1) | async-done | bytes 327712 | tf_op jit(solution)/shard_map/all_to_all | solution.py:452
  38.5 38.9 %first_sweep.1 = (f32[16,128]{1,0:T(8,128)S(1)}, f32[16,128]{1,0:T(8,128)S(1)}, f32[32,128]{1,0:T(8,128)S(1)}, bf16[2080,128]{1,0:T(8,128)(2,1)S(1)}) custom-call(s32[1]{0:T(128)} %get-tuple-element.14.refs_0_, s32[1]{0:T(128)} %bitcast.1.own_ref.refs_1_, bf16[16,40,256]{2,1,0:T(8,128)(2,1)S(1)} %all-to-all-done.1.refs_2_, ...), custom_call_target="tpu_custom_call" | custom-call | tf_op jit(solution)/shard_map/first_sweep/pallas_call | solution.py:415
  77.5 1.6 %collective-permute-start = (f32[16,128]{1,0:T(8,128)S(1)}, f32[16,128]{1,0:T(8,128)S(1)}, u32[]{:S(2)}, u32[]{:S(2)}) collective-permute-start(f32[16,128]{1,0:T(8,128)S(1)} %get-tuple-element.18), channel_id=1, source_target_pairs={{0,1},{1,0},{2,3},{3,2},{4,5},{5,4},{6,7},{7,6},{8,9},{9,8},{10,11... | collective-permute-start | bytes 24584 | tf_op jit(solution)/shard_map/ppermute | solution.py:456
  79.1 0.8 collective-permute-done.other_ref
  79.9 9.9 %all_to_all.31.parts_ref = f32[16,16,128]{2,1,0:T(8,128)S(1)} all-to-all(f32[16,16,128]{2,1,0:T(8,128)S(1)} %merge_pair.2), channel_id=1, replica_groups=mesh['state'=16,'sample'=16] {'state'}, dimensions={0} | all-to-all | bytes 262144 | tf_op jit(solution)/shard_map/all_to_all | solution.py:452
  89.9 13.4 %all_to_all.32 = f32[16,16,128]{2,1,0:T(8,128)S(1)} all-to-all(f32[16,16,128]{2,1,0:T(8,128)S(1)} %merge.2), channel_id=1, replica_groups=mesh['state'=16,'sample'=16] {'sample'}, dimensions={0} | all-to-all | bytes 262144 | tf_op jit(solution)/shard_map/all_to_all | solution.py:452
  103.2 4.9 %next_sweep.1 = (f32[16,128]{1,0:T(8,128)S(1)}, f32[16,128]{1,0:T(8,128)S(1)}, f32[32,128]{1,0:T(8,128)S(1)}) custom-call(s32[1]{0:T(128)} %get-tuple-element.14.refs_0_, s32[1]{0:T(128)} %bitcast.1.own_ref.refs_1_, bf16[16,40,256]{2,1,0:T(8,128)(2,1)S(1)} %all-to-all-done.1.refs_2_, bf16[2080,128]{1,0:T(8,128)(2,1)S(1)} %get-tuple-element.16.refs_3_, ...), custom_call_target="tpu_custom_call" | custom-call | tf_op jit(solution)/shard_map/next_sweep/pallas_call | solution.py:415
  108.2 0.1 collective-permute-start.1
  108.3 1.2 collective-permute-done.1.other_ref
  109.5 9.9 %all_to_all.33.parts_ref = f32[16,16,128]{2,1,0:T(8,128)S(1)} all-to-all(f32[16,16,128]{2,1,0:T(8,128)S(1)} %merge_pair.3), channel_id=1, replica_groups=mesh['state'=16,'sample'=16] {'state'}, dimensions={0} | all-to-all | bytes 262144 | tf_op jit(solution)/shard_map/all_to_all | solution.py:452
  119.4 13.2 %all_to_all.34 = f32[16,16,128]{2,1,0:T(8,128)S(1)} all-to-all(f32[16,16,128]{2,1,0:T(8,128)S(1)} %merge.3), channel_id=1, replica_groups=mesh['state'=16,'sample'=16] {'sample'}, dimensions={0} | all-to-all | bytes 262144 | tf_op jit(solution)/shard_map/all_to_all | solution.py:452
  132.5 0.7 finish.1
  (4 shorter events, 0.1 us)
Async XLA Ops:
  0.0 22.4 %copy-start.1 = (f32[256]{0:T(256)S(1)}, f32[256]{0:T(256)}, u32[]{:S(2)}) copy-start(f32[256]{0:T(256)} %param.7) | copy-start | bytes 3076
  0.0 22.4 %copy-start = (bf16[32,256]{1,0:T(8,128)(2,1)S(1)}, bf16[32,256]{1,0:T(8,128)(2,1)}, u32[]{:S(2)}) copy-start(bf16[32,256]{1,0:T(8,128)(2,1)} %coef_ref.1) | copy-start | bytes 49156
  23.2 15.4 %all-to-all-start.1 = ((bf16[16,40,256]{2,1,0:T(8,128)(2,1)}), bf16[16,40,256]{2,1,0:T(8,128)(2,1)S(1)}, u32[]{:S(2)}, u32[]{:S(2)}) async-start(bf16[16,40,256]{2,1,0:T(8,128)(2,1)} %pack.1), calls=%async_computation.1 | async-start | bytes 655360 | tf_op jit(solution)/shard_map/all_to_all | solution.py:452
  77.5 2.4 %collective-permute-start = (f32[16,128]{1,0:T(8,128)S(1)}, f32[16,128]{1,0:T(8,128)S(1)}, u32[]{:S(2)}, u32[]{:S(2)}) collective-permute-start(f32[16,128]{1,0:T(8,128)S(1)} %get-tuple-element.18), channel_id=1, source_target_pairs={{0,1},{1,0},{2,3},{3,2},{4,5},{5,4},{6,7},{7,6},{8,9},{9,8},{10,11... | collective-permute-start | bytes 24584 | tf_op jit(solution)/shard_map/ppermute | solution.py:456
  108.2 1.3 collective-permute-start.1

commit v9 on v8

--- a/solution.py
+++ b/solution.py
@@ -151,7 +151,7 @@
 
 
 def arrange(group, own, pieces):
-    most = pl.cdiv(pieces.shape[0] * LANES, ROW_TILE) * ROW_TILE
+    most = pl.cdiv(pieces.shape[0] * LANES, 2 * ROW_TILE) * 2 * ROW_TILE
     smem = pl.BlockSpec(memory_space=pltpu.SMEM)
     vmem = pl.BlockSpec(memory_space=pltpu.VMEM)
     return pl.pallas_call(
@@ -240,11 +240,13 @@
 
 def sweep_kernel(first, *refs):
     if first:
-        amount_ref, own_ref, packed_ref, left_ref, kept_ref, sent_ref, wide_ref, shifted_ref, right_ref, scaled_ref, acc_ref, some_ref, tall_ref, top_ref = refs
+        amount_ref, own_ref, packed_ref, left_ref, kept_ref, sent_ref, wide_ref, shifted_ref, right_ref, even_ref, odd_ref, even_share_ref, odd_share_ref, acc_ref, some_ref, tall_ref, top_ref = refs
         source_ref = shifted_ref
     else:
-        amount_ref, own_ref, packed_ref, left_ref, parts_ref, old_ref, kept_ref, sent_ref, wide_ref, some_ref, right_ref, scaled_ref, acc_ref, tall_ref, top_ref = refs
+        amount_ref, own_ref, packed_ref, left_ref, parts_ref, old_ref, kept_ref, sent_ref, wide_ref, some_ref, right_ref, even_ref, odd_ref, even_share_ref, odd_share_ref, acc_ref, tall_ref, top_ref = refs
         source_ref = left_ref
+    scaled_refs = (even_ref, odd_ref)
+    share_refs = (even_share_ref, odd_share_ref)
     groups, packed_rows, _ = packed_ref.shape
     components = packed_rows - 8
     states = groups * STATE_TILE
@@ -302,7 +304,7 @@
         chosen = jnp.logical_and(lane >= SHIFT_AT, lane < LIVE_AT)
         return jnp.where(chosen, values, block.astype(jnp.float32)).astype(jnp.bfloat16)
 
-    def visit(t, carry):
+    def begin(t, slot, carry, beside):
         least, most = carry
         rows = pl.ds(pl.multiple_of(t * ROW_TILE, ROW_TILE), ROW_TILE)
         left = left_ref[rows, :]
@@ -315,22 +317,32 @@
         for g in range(groups):
             lanes = slice(g * STATE_TILE, (g + 1) * STATE_TILE)
             scaled = jnp.exp2(product(left, right_ref[:, lanes]))
-            scaled_ref[:, lanes] = scaled
+            scaled_refs[slot][:, lanes] = scaled
             total += folded(scaled, jnp.add)
+            beside(g)
         denominator = jnp.sum(total, axis=1, keepdims=True)
         least = jnp.minimum(least, jnp.where(live > 0.0, denominator, 1.0))
         most = jnp.maximum(most, jnp.where(live > 0.0, denominator, 1.0))
-        share = jnp.broadcast_to(live / denominator, (ROW_TILE, LANES))
+        share_refs[slot][...] = jnp.broadcast_to(live / denominator, (ROW_TILE, LANES))
         if first:
             shifted_ref[rows, :] = shifted(left, shift + jnp.log2(denominator))
-        for k in range(states // LANES):
-            lanes = slice(k * LANES, (k + 1) * LANES)
-            part = scaled_ref[:, lanes] * share
+        return least, most
+
+    def end(slot, g):
+        for h in range(pair):
+            lanes = slice((pair * g + h) * LANES, (pair * g + h + 1) * LANES)
+            part = scaled_refs[slot][:, lanes] * share_refs[slot][...]
             acc_ref[:, lanes] += jnp.sum(part.reshape(ROW_TILE // 8, 8, LANES), axis=0)
-        return least, most
+
+    def visit(t, carry):
+        carry = begin(2 * t, 0, carry, lambda g: None)
+        carry = begin(2 * t + 1, 1, carry, lambda g: end(0, g))
+        for g in range(groups):
+            end(1, g)
+        return carry
 
     unit = jnp.ones((ROW_TILE, 1), jnp.float32)
-    least, most = lax.fori_loop(0, tiles, visit, (unit, unit))
+    least, most = lax.fori_loop(0, (tiles + 1) // 2, visit, (unit, unit))
     least = jnp.min(least, axis=0, keepdims=True)
     most = jnp.max(most, axis=0, keepdims=True)
     sums = jnp.sum(acc_ref[...], axis=0, keepdims=True)
@@ -403,6 +415,9 @@
     scratch = [
         pltpu.VMEM((DEPTH, states), jnp.bfloat16),
         pltpu.VMEM((ROW_TILE, states), jnp.float32),
+        pltpu.VMEM((ROW_TILE, states), jnp.float32),
+        pltpu.VMEM((ROW_TILE, LANES), jnp.float32),
+        pltpu.VMEM((ROW_TILE, LANES), jnp.float32),
         pltpu.VMEM((8, states), jnp.float32),
         pltpu.VMEM((DEPTH, 2 * LANES), jnp.bfloat16),
         pltpu.VMEM((tall, LANES), jnp.float32),
@@ -411,13 +426,13 @@
     if first:
         outs.append((left.shape, jnp.bfloat16))
     else:
-        scratch = [scratch[3]] + scratch[:3] + scratch[4:]
+        scratch = [scratch[6]] + scratch[:6] + scratch[7:]
     return pl.pallas_call(
         functools.partial(sweep_kernel, first),
         out_shape=[jax.ShapeDtypeStruct(*out) for out in outs],
         in_specs=[pl.BlockSpec(memory_space=pltpu.SMEM)] * 2 + [pl.BlockSpec(memory_space=pltpu.VMEM)] * (len(operands) - 2),
         scratch_shapes=scratch,
-        compiler_params=pltpu.CompilerParams(vmem_limit_bytes=20 * 2**20),
+        compiler_params=pltpu.CompilerParams(vmem_limit_bytes=28 * 2**20),
         name="first_sweep" if first else "next_sweep",
     )(*operands)
 

time: 134 us -> 134 us (level)
  no operation moved by 1% of the time
where the time goes in v9:
time: 134 us; the launch traced here: 133 us
  blocking collectives  65.7 us (49%)
  Pallas kernels  49.2 us (37%)
  waiting for transfers between devices  9.71 us (7%)
  starting transfers between devices  8.44 us (6%)
    all_to_all x5, blocking collectives, spread(): return lax.all_to_all(copies, axis, 0, 0)  65.7 us
    pallas_call x2, Pallas kernels, sweep(): pl.pallas_call(functools.partial(sweep_kernel, first), out_shape=[jax.Sha...  43.7 us
    all_to_all x1, waiting for transfers between devices, spread(): return lax.all_to_all(copies, axis, 0, 0)  7.72 us
    all_to_all x1, starting transfers between devices, spread(): return lax.all_to_all(copies, axis, 0, 0)  6.75 us
    pallas_call x1, Pallas kernels, prepare(): pl.pallas_call(prepare_kernel, out_shape=jax.ShapeDtypeStruct((copies, co...  2.95 us
  transfers between devices with their start and end apart: 3, of which 3 were waited for; matrix products, arithmetic and copies ran while one was open for 0% of the time, Pallas kernels for 1%

profile of v9, /device:TPU:1, one launch (start us, length us, event | category | flops | bytes accessed | tf_op | source)
XLA Modules:
  0.0 133.1 jit_solution(7781040260433083824)
XLA Ops:
  0.0 0.0 copy-start.1
  0.0 0.0 copy-start
  0.0 3.0 %prepare.1 = bf16[16,40,128]{2,1,0:T(8,128)(2,1)S(1)} custom-call(s32[1]{0:T(128)} %bitcast.group_ref, s32[1,32768]{1,0:T(1,128)} %bitcast.10, bf16[32,32768]{1,0:T(8,128)(2,1)} %energy_ref.1), custom_call_target="tpu_custom_call" | custom-call | tf_op jit(solution)/shard_map/prepare/pallas_call | solution.py:112
  3.0 19.4 %all_to_all.30.pieces_ref = bf16[16,40,128]{2,1,0:T(8,128)(2,1)S(1)} all-to-all(bf16[16,40,128]{2,1,0:T(8,128)(2,1)S(1)} %prepare.1), channel_id=1, replica_groups=mesh['state'=16,'sample'=16] {'sample'}, dimensions={0} | all-to-all | bytes 327680 | tf_op jit(solution)/shard_map/all_to_all | solution.py:467
  22.4 0.0 copy-done.1
  22.4 0.0 copy-done
  22.4 0.8 pack.1
  23.2 6.8 %all-to-all-start.1 = ((bf16[16,40,256]{2,1,0:T(8,128)(2,1)}), bf16[16,40,256]{2,1,0:T(8,128)(2,1)S(1)}, u32[]{:S(2)}, u32[]{:S(2)}) async-start(bf16[16,40,256]{2,1,0:T(8,128)(2,1)} %pack.1), calls=%async_computation.1 | async-start | bytes 655360 | tf_op jit(solution)/shard_map/all_to_all | solution.py:467
  29.9 0.9 arrange.1
  30.8 7.7 %all-to-all-done.1.refs_2_ = bf16[16,40,256]{2,1,0:T(8,128)(2,1)S(1)} async-done(((bf16[16,40,256]{2,1,0:T(8,128)(2,1)}), bf16[16,40,256]{2,1,0:T(8,128)(2,1)S(1)}, u32[]{:S(2)}, u32[]{:S(2)}) %all-to-all-start.1) | async-done | bytes 327712 | tf_op jit(solution)/shard_map/all_to_all | solution.py:467
  38.5 38.8 %first_sweep.1 = (f32[16,128]{1,0:T(8,128)S(1)}, f32[16,128]{1,0:T(8,128)S(1)}, f32[32,128]{1,0:T(8,128)S(1)}, bf16[2496,128]{1,0:T(8,128)(2,1)S(1)}) custom-call(s32[1]{0:T(128)} %get-tuple-element.14.refs_0_, s32[1]{0:T(128)} %bitcast.1.own_ref.refs_1_, bf16[16,40,256]{2,1,0:T(8,128)(2,1)S(1)} %all-to-all-done.1.refs_2_, ...), custom_call_target="tpu_custom_call" | custom-call | tf_op jit(solution)/shard_map/first_sweep/pallas_call | solution.py:430
  77.4 1.6 %collective-permute-start = (f32[16,128]{1,0:T(8,128)S(1)}, f32[16,128]{1,0:T(8,128)S(1)}, u32[]{:S(2)}, u32[]{:S(2)}) collective-permute-start(f32[16,128]{1,0:T(8,128)S(1)} %get-tuple-element.18), channel_id=1, source_target_pairs={{0,1},{1,0},{2,3},{3,2},{4,5},{5,4},{6,7},{7,6},{8,9},{9,8},{10,11... | collective-permute-start | bytes 24584 | tf_op jit(solution)/shard_map/ppermute | solution.py:471
  79.0 0.8 collective-permute-done.other_ref
  79.8 9.9 %all_to_all.31.parts_ref = f32[16,16,128]{2,1,0:T(8,128)S(1)} all-to-all(f32[16,16,128]{2,1,0:T(8,128)S(1)} %merge_pair.2), channel_id=1, replica_groups=mesh['state'=16,'sample'=16] {'state'}, dimensions={0} | all-to-all | bytes 262144 | tf_op jit(solution)/shard_map/all_to_all | solution.py:467
  89.8 13.4 %all_to_all.32 = f32[16,16,128]{2,1,0:T(8,128)S(1)} all-to-all(f32[16,16,128]{2,1,0:T(8,128)S(1)} %merge.2), channel_id=1, replica_groups=mesh['state'=16,'sample'=16] {'sample'}, dimensions={0} | all-to-all | bytes 262144 | tf_op jit(solution)/shard_map/all_to_all | solution.py:467
  103.2 4.9 %next_sweep.1 = (f32[16,128]{1,0:T(8,128)S(1)}, f32[16,128]{1,0:T(8,128)S(1)}, f32[32,128]{1,0:T(8,128)S(1)}) custom-call(s32[1]{0:T(128)} %get-tuple-element.14.refs_0_, s32[1]{0:T(128)} %bitcast.1.own_ref.refs_1_, bf16[16,40,256]{2,1,0:T(8,128)(2,1)S(1)} %all-to-all-done.1.refs_2_, bf16[2496,128]{1,0:T(8,128)(2,1)S(1)} %get-tuple-element.16.refs_3_, ...), custom_call_target="tpu_custom_call" | custom-call | tf_op jit(solution)/shard_map/next_sweep/pallas_call | solution.py:430
  108.1 0.1 collective-permute-start.1
  108.2 1.2 collective-permute-done.1.other_ref
  109.3 9.9 %all_to_all.33.parts_ref = f32[16,16,128]{2,1,0:T(8,128)S(1)} all-to-all(f32[16,16,128]{2,1,0:T(8,128)S(1)} %merge_pair.3), channel_id=1, replica_groups=mesh['state'=16,'sample'=16] {'state'}, dimensions={0} | all-to-all | bytes 262144 | tf_op jit(solution)/shard_map/all_to_all | solution.py:467
  119.3 13.2 %all_to_all.34 = f32[16,16,128]{2,1,0:T(8,128)S(1)} all-to-all(f32[16,16,128]{2,1,0:T(8,128)S(1)} %merge.3), channel_id=1, replica_groups=mesh['state'=16,'sample'=16] {'sample'}, dimensions={0} | all-to-all | bytes 262144 | tf_op jit(solution)/shard_map/all_to_all | solution.py:467
  132.4 0.7 finish.1
  (4 shorter events, 0.1 us)
Async XLA Ops:
  0.0 22.4 %copy-start.1 = (f32[256]{0:T(256)S(1)}, f32[256]{0:T(256)}, u32[]{:S(2)}) copy-start(f32[256]{0:T(256)} %param.7) | copy-start | bytes 3076
  0.0 22.4 %copy-start = (bf16[32,256]{1,0:T(8,128)(2,1)S(1)}, bf16[32,256]{1,0:T(8,128)(2,1)}, u32[]{:S(2)}) copy-start(bf16[32,256]{1,0:T(8,128)(2,1)} %coef_ref.1) | copy-start | bytes 49156
  23.2 15.4 %all-to-all-start.1 = ((bf16[16,40,256]{2,1,0:T(8,128)(2,1)}), bf16[16,40,256]{2,1,0:T(8,128)(2,1)S(1)}, u32[]{:S(2)}, u32[]{:S(2)}) async-start(bf16[16,40,256]{2,1,0:T(8,128)(2,1)} %pack.1), calls=%async_computation.1 | async-start | bytes 655360 | tf_op jit(solution)/shard_map/all_to_all | solution.py:467
  77.4 2.4 %collective-permute-start = (f32[16,128]{1,0:T(8,128)S(1)}, f32[16,128]{1,0:T(8,128)S(1)}, u32[]{:S(2)}, u32[]{:S(2)}) collective-permute-start(f32[16,128]{1,0:T(8,128)S(1)} %get-tuple-element.18), channel_id=1, source_target_pairs={{0,1},{1,0},{2,3},{3,2},{4,5},{5,4},{6,7},{7,6},{8,9},{9,8},{10,11... | collective-permute-start | bytes 24584 | tf_op jit(solution)/shard_map/ppermute | solution.py:471
  108.1 1.3 collective-permute-start.1
